TPU v7x, 128 devices: a whole 4x4x4 slice. The times are simulated.
128 devices in a mesh: alpha: 16 (over z, y), beta: 8 (over x, core).
Axes of the slice: x: 4, y: 4, z: 4, core: 2. Of those that a mesh axis runs over, the one named last changes fastest.
Arguments:
- ci_vector: float32 [2048, 2048], P('alpha', 'beta'), may hold values from -6 to 6
- one_body: float32 [102], replicated, may hold values from -1 to 1
- pair_integrals: bfloat16 [102, 102], replicated, may hold values from -0.15625 to 0.15625
- beta_target: int32 [40, 2048], P(None, 'beta'), may hold values from 0 to 2047
- beta_pair: int32 [40, 2048], P(None, 'beta'), may hold values from 0 to 101
- beta_sign: int32 [40, 2048], P(None, 'beta'), may hold values 0 or 1
- alpha_target: int32 [40, 2048], P(None, 'alpha'), may hold values from 0 to 2047
- alpha_pair: int32 [40, 2048], P(None, 'alpha'), may hold values from 0 to 101
- alpha_sign: int32 [40, 2048], P(None, 'alpha'), may hold values 0 or 1
Outputs:
- sigma_vector: float32 [2048, 2048], P('alpha', 'beta')
All inputs are finite; a program needn't handle non-finite values. No bound on the sum of `beta_sign` or of `alpha_sign` on one device may be relied on, other than what follows from the above.
Results may differ from a plain program's by a relative error of at most 0.0035.
Values may be sent and summed in bfloat16 or wider, within the bound.
A program may use at most 128 MiB of HBM per device.

v0:
```python
import jax
import jax.numpy as jnp
from jax import lax
from jax.sharding import PartitionSpec as P

precise = lax.Precision.HIGHEST


def sent_to_all(value, axis):
    copies = jnp.broadcast_to(value, (lax.axis_size(axis), *value.shape))
    return lax.all_to_all(copies, axis, split_axis=0, concat_axis=0, tiled=True)


def in_order(parts, dim):
    parts = jnp.moveaxis(parts, 0, dim)
    shape = parts.shape
    return parts.reshape(*shape[:dim], shape[dim] * shape[dim + 1], *shape[dim + 2 :])


def gathered_copies(value, axis, dim):
    parts = sent_to_all(value, axis)
    return in_order(parts, dim)


def in_blocks(value, dim, size):
    before, after = (value.shape[:dim], value.shape[dim + 1 :])
    return jnp.moveaxis(value.reshape(*before, size, -1, *after), dim, 0)


def summed_on_arrival(value, axis, dim):
    parts = in_blocks(value, dim, lax.axis_size(axis))
    arrived = lax.all_to_all(parts, axis, split_axis=0, concat_axis=0, tiled=True)
    return arrived.sum(axis=0)


def shards(
    ci_vector,
    one_body,
    pair_integrals,
    beta_target,
    beta_pair,
    beta_sign,
    alpha_target,
    alpha_pair,
    alpha_sign,
):
    alpha_count = ci_vector.shape[0]
    beta_count = ci_vector.shape[1]
    pair_count = one_body.shape[0]
    total_alpha = alpha_count * lax.axis_size("alpha")
    civec_bf = ci_vector.astype(jnp.bfloat16)
    rows_whole = gathered_copies(civec_bf, "beta", 1)
    total_beta = rows_whole.shape[1]
    pair_ids = jnp.arange(pair_count, dtype=jnp.int32)
    beta_hot = (
        (2 * beta_sign - 1)[:, :, None] * (beta_pair[:, :, None] == pair_ids).astype(jnp.int32)
    ).astype(jnp.bfloat16)
    alpha_signed = (2 * alpha_sign - 1)[:, :, None] * (alpha_pair[:, :, None] == pair_ids).astype(
        jnp.int32
    )
    alpha_hot = alpha_signed.astype(jnp.bfloat16)
    alpha_level = jnp.einsum(
        "eaq,q->ea", alpha_signed.astype(jnp.float32), one_body, precision=precise
    )
    col_block = min(128, beta_count)
    col_blocks = beta_count // col_block
    string_ids = jnp.arange(total_beta, dtype=jnp.int32)

    def beta_block(block_index):
        start = block_index * col_block
        targets = lax.dynamic_slice_in_dim(beta_target, start, col_block, 1)
        hot_cols = lax.dynamic_slice_in_dim(beta_hot, start, col_block, 1)
        coupling = (targets[None, :, :] == string_ids[:, None, None]).astype(jnp.bfloat16)
        picked = jnp.einsum(
            "aj,jei->aei", rows_whole, coupling, preferred_element_type=jnp.float32
        ).astype(jnp.bfloat16)
        return jnp.einsum("aei,eip->pai", picked, hot_cols, preferred_element_type=jnp.float32)

    blocks = lax.map(beta_block, jnp.arange(col_blocks, dtype=jnp.int32))
    density = jnp.transpose(blocks, (1, 2, 0, 3)).reshape(pair_count, alpha_count, beta_count)
    same_beta = jnp.einsum("p,pai->ai", one_body, density, precision=precise)
    density_bf = density.astype(jnp.bfloat16)
    mixed = jnp.einsum(
        "qp,pai->qai", pair_integrals, density_bf, preferred_element_type=jnp.float32
    ).astype(jnp.bfloat16)
    alpha_ids = jnp.arange(total_alpha, dtype=jnp.int32)
    block_rows = 32

    def accumulate(partial_value, block_index):
        offset = block_index * block_rows
        hot_rows = lax.dynamic_slice_in_dim(alpha_hot, offset, block_rows, 1)
        mixed_rows = lax.dynamic_slice_in_dim(mixed, offset, block_rows, 1)
        lifted_bf = jnp.einsum(
            "eaq,qai->aei", hot_rows, mixed_rows, preferred_element_type=jnp.float32
        ).astype(jnp.bfloat16)
        targets = lax.dynamic_slice_in_dim(alpha_target, offset, block_rows, 1)
        matches = targets.T[None, :, :] == alpha_ids[:, None, None]
        spread = matches.astype(jnp.bfloat16)
        partial_value = partial_value + jnp.einsum(
            "bae,aei->bi", spread, lifted_bf, preferred_element_type=jnp.float32
        )
        level_rows = lax.dynamic_slice_in_dim(alpha_level, offset, block_rows, 1)
        level_map = jnp.sum(jnp.where(matches, level_rows.T[None, :, :], jnp.float32(0.0)), axis=2)
        own_block = lax.dynamic_slice_in_dim(civec_bf, offset, block_rows, 0).astype(jnp.float32)
        partial_value = partial_value + jnp.dot(level_map, own_block, precision=precise)
        return (partial_value, None)

    partial_value, unused = lax.scan(
        accumulate,
        jnp.zeros((total_alpha, beta_count), jnp.float32),
        jnp.arange(alpha_count // block_rows, dtype=jnp.int32),
    )
    own_rows = summed_on_arrival(partial_value, "alpha", 0)
    return own_rows + same_beta


def solution(mesh):
    placed = (
        P("alpha", "beta"),
        P(),
        P(),
        P(None, "beta"),
        P(None, "beta"),
        P(None, "beta"),
        P(None, "alpha"),
        P(None, "alpha"),
        P(None, "alpha"),
    )
    return jax.shard_map(
        shards, mesh=mesh, in_specs=placed, out_specs=P("alpha", "beta"), check_vma=False
    )
```

profile of v0, /device:TPU:1, one launch (start us, length us, event | category | flops | bytes accessed | tf_op | source)
XLA Modules:
  0.0 169.8 jit_solution(2291118660412104876)
XLA Ops:
  0.0 0.9 convert_element_type.37
  0.9 0.8 broadcast_in_dim.38
  1.8 5.8 %all-to-all-start = ((bf16[8,128,256]{2,1,0:T(8,128)(2,1)}), bf16[8,128,256]{2,1,0:T(8,128)(2,1)S(1)}, u32[]{:S(2)}, u32[]{:S(2)}) async-start(bf16[8,128,256]{2,1,0:T(8,128)(2,1)} %broadcast_in_dim.38), calls=%async_computation | async-start | bytes 1048576 | tf_op jit(solution)/shard_map/all_to_all | solution.py:11
  7.6 0.8 multiply_add_fusion
  8.4 0.9 copy.22
  9.3 0.7 multiply_add_fusion.1
  10.2 0.8 copy.20
  11.0 1.5 copy.28
  12.4 3.9 %select_convert_fusion.2 = bf16[40,128,102]{2,0,1:T(8,128)(2,1)} fusion(s32[40,128]{0,1:T(8,128)S(1)} %copy.21, s32[40,128]{0,1:T(8,128)S(1)} %copy.20), kind=kLoop, calls=%fused_computation.35 | loop fusion | flops 1566720 | bytes 1085440 | tf_op jit(solution)/shard_map/convert_element_type | solution.py:61
  16.3 3.5 %fusion.37 = f32[40,128]{0,1:T(8,128)} fusion(f32[102]{0:T(128)S(1)} %copy-done.2, s32[40,128]{0,1:T(8,128)S(1)} %copy.21, s32[40,128]{0,1:T(8,128)S(1)} %copy.20), kind=kLoop, calls=%fused_computation.38 | loop fusion | flops 2606080 | bytes 61848 | tf_op jit(solution)/shard_map/eaq,q->ea/dot_general | solution.py:62
  19.9 3.9 %select_convert_fusion = bf16[40,256,102]{2,0,1:T(8,128)(2,1)S(1)} fusion(s32[40,256]{0,1:T(8,128)S(1)} %copy.23, s32[40,256]{0,1:T(8,128)S(1)} %copy.22), kind=kLoop, calls=%fused_computation.32 | loop fusion | flops 3133440 | bytes 2170880 | tf_op jit(solution)/shard_map/convert_element_type | solution.py:57
  23.8 1.0 copy.24
  24.8 2.0 %copy.26 = bf16[128,2048]{1,0:T(8,128)(2,1)} copy(bf16[128,2048]{0,1:T(8,128)(2,1)} %bitcast.69) | data formatting | bytes 1048576
  26.8 30.6 %while.22 = (s32[]{:T(128)}, f32[2,102,128,128]{2,1,3,0:T(8,128)}, s32[2]{0:T(128)S(1)}, bf16[40,256,102]{2,0,1:T(8,128)(2,1)S(1)}, s32[40,256]{1,0:T(8,128)S(1)...) while((s32[]{:T(128)}, f32[2,102,128,128]{2,1,3,0:T(8,128)}, ...), condition=%wide.region_1.2_spmd.clone, body=%wide.region_0.1_spmd.clone.sunk | while | flops 2829189120 | bytes 8798887 | solution.py:79
  26.8 0.6 dynamic_slice.65
  28.2 13.9 %bitcast_dynamic-update-slice_fusion.2 = f32[2,102,128,128]{2,1,3,0:T(8,128)} fusion(f32[2,102,128,128]{2,1,3,0:T(8,128)} %get-tuple-element.289, s32[]{:T(128)} %get-tuple-element.288, s32[40,128]{0,1:T(8,128)S(1)} %copy.37, bf16[40,256,102]{2,0,1:T(8,128)(2,1)S(1)} %get-tuple-element.301, s32[]{:T(128)S(6)} %select_n.24, ...), kind=kOutput, calls=%fused_computation.5.clone.1 | convolution fusion | flops 2829189120 | bytes 8716804 | tf_op jit(solution)/shard_map/while/body/eval_jaxpr/aei,eip->pai/dot_general | solution.py:77
  42.1 0.6 dynamic_slice.65
  43.5 14.0 %bitcast_dynamic-update-slice_fusion.2 = f32[2,102,128,128]{2,1,3,0:T(8,128)} fusion(f32[2,102,128,128]{2,1,3,0:T(8,128)} %get-tuple-element.289, s32[]{:T(128)} %get-tuple-element.288, s32[40,128]{0,1:T(8,128)S(1)} %copy.37, bf16[40,256,102]{2,0,1:T(8,128)(2,1)S(1)} %get-tuple-element.301, s32[]{:T(128)S(6)} %select_n.24, ...), kind=kOutput, calls=%fused_computation.5.clone.1 | convolution fusion | flops 2829189120 | bytes 8716804 | tf_op jit(solution)/shard_map/while/body/eval_jaxpr/aei,eip->pai/dot_general | solution.py:77
  57.5 12.9 %copy.27 = bf16[102,128,256]{2,0,1:T(8,128)(2,1)} copy(f32[102,128,256]{1,0,2:T(8,128)} %bitcast.66) | data formatting | bytes 20054016 | tf_op jit(solution)/shard_map/reshape | solution.py:80
  70.3 7.6 %fusion.32 = bf16[102,128,256]{2,0,1:T(8,128)(2,1)} fusion(bf16[102,128,256]{2,0,1:T(8,128)(2,1)} %copy.27, bf16[102,102]{1,0:T(8,128)(2,1)S(1)} %copy-done), kind=kOutput, calls=%fused_computation.31 | convolution fusion | flops 685178880 | bytes 13390152 | tf_op jit(solution)/shard_map/qp,pai->qai/dot_general | solution.py:83
  77.9 49.9 %while.23 = (s32[]{:T(128)}, f32[2048,256]{1,0:T(8,128)}, s32[4]{0:T(128)S(1)}, s32[40,128]{0,1:T(8,128)}, bf16[40,128,102]{2,0,1:T(8,128)(2,1)}, /*index=5*/bf1...) while((s32[]{:T(128)}, f32[2048,256]{1,0:T(8,128)}, ...), condition=%wide.region_4.5_spmd.clone, body=%wide.region_2.4_spmd.clone.sunk | while | flops 1622671360 | bytes 10998468 | solution.py:108
  77.9 0.6 dynamic_slice.71
  79.1 0.7 dynamic-slice_bitcast_fusion.4
  79.8 4.8 %fusion.58 = f32[2048,256]{1,0:T(8,128)S(1)} fusion(s32[32,40]{1,0:T(8,128)S(1)} %dynamic-slice_bitcast_fusion.4, f32[2048,256]{1,0:T(8,128)} %get-tuple-element.321, bf16[102,128,256]{2,0,1:T(8,128)(2,1)} %get-tuple-element.337, s32[]{:T(128)S(6)} %select_n.26, pred[]{:T(512)S(6)} %compare.3, bf16[40,128,102]{2,0,1:T(8,128)(2,1)} %get-tuple-element.336), kind=kOutput, calls=%fused_computation.19.clone.1 | convolution fusion | flops 1413021696 | bytes 6232576 | tf_op jit(solution)/shard_map/while/body/eval_jaxpr/bae,aei->bi/dot_general | solution.py:99
  84.6 0.7 dynamic-slice_bitcast_fusion.5
  85.3 2.2 %fusion.59 = f32[2048,32]{0,1:T(8,128)S(1)} fusion(f32[32,40]{1,0:T(8,128)S(1)} %dynamic-slice_bitcast_fusion.5, s32[32,40]{1,0:T(8,128)S(1)} %dynamic-slice_bitcast_fusion.4), kind=kLoop, calls=%fused_computation.15.clone.1 | loop fusion | flops 7798784 | bytes 272384 | tf_op jit(solution)/shard_map/while/body/eval_jaxpr/reduce_sum | solution.py:103
  87.6 2.3 %convolution_add_fusion.2 = f32[2048,256]{1,0:T(8,128)} fusion(f32[2048,256]{1,0:T(8,128)S(1)} %fusion.58, f32[2048,32]{0,1:T(8,128)S(1)} %fusion.59, bf16[128,256]{1,0:T(8,128)(2,1)S(1)} %get-tuple-element.339, s32[]{:T(128)S(6)} %select_n.26), kind=kOutput, calls=%fused_computation.18.clone.1 | convolution fusion | flops 201850880 | bytes 4472836 | tf_op jit(solution)/shard_map/while/body/eval_jaxpr/dot_general | solution.py:105
  89.9 0.6 dynamic_slice.71
  91.1 0.7 dynamic-slice_bitcast_fusion.4
  91.8 5.4 %fusion.58 = f32[2048,256]{1,0:T(8,128)S(1)} fusion(s32[32,40]{1,0:T(8,128)S(1)} %dynamic-slice_bitcast_fusion.4, f32[2048,256]{1,0:T(8,128)} %get-tuple-element.321, bf16[102,128,256]{2,0,1:T(8,128)(2,1)} %get-tuple-element.337, s32[]{:T(128)S(6)} %select_n.26, pred[]{:T(512)S(6)} %compare.3, bf16[40,128,102]{2,0,1:T(8,128)(2,1)} %get-tuple-element.336), kind=kOutput, calls=%fused_computation.19.clone.1 | convolution fusion | flops 1413021696 | bytes 6232576 | tf_op jit(solution)/shard_map/while/body/eval_jaxpr/bae,aei->bi/dot_general | solution.py:99
  97.2 0.7 dynamic-slice_bitcast_fusion.5
  98.0 2.2 %fusion.59 = f32[2048,32]{0,1:T(8,128)S(1)} fusion(f32[32,40]{1,0:T(8,128)S(1)} %dynamic-slice_bitcast_fusion.5, s32[32,40]{1,0:T(8,128)S(1)} %dynamic-slice_bitcast_fusion.4), kind=kLoop, calls=%fused_computation.15.clone.1 | loop fusion | flops 7798784 | bytes 272384 | tf_op jit(solution)/shard_map/while/body/eval_jaxpr/reduce_sum | solution.py:103
  100.2 2.3 %convolution_add_fusion.2 = f32[2048,256]{1,0:T(8,128)} fusion(f32[2048,256]{1,0:T(8,128)S(1)} %fusion.58, f32[2048,32]{0,1:T(8,128)S(1)} %fusion.59, bf16[128,256]{1,0:T(8,128)(2,1)S(1)} %get-tuple-element.339, s32[]{:T(128)S(6)} %select_n.26), kind=kOutput, calls=%fused_computation.18.clone.1 | convolution fusion | flops 201850880 | bytes 4472836 | tf_op jit(solution)/shard_map/while/body/eval_jaxpr/dot_general | solution.py:105
  102.5 0.6 dynamic_slice.71
  103.7 0.7 dynamic-slice_bitcast_fusion.4
  104.4 5.4 %fusion.58 = f32[2048,256]{1,0:T(8,128)S(1)} fusion(s32[32,40]{1,0:T(8,128)S(1)} %dynamic-slice_bitcast_fusion.4, f32[2048,256]{1,0:T(8,128)} %get-tuple-element.321, bf16[102,128,256]{2,0,1:T(8,128)(2,1)} %get-tuple-element.337, s32[]{:T(128)S(6)} %select_n.26, pred[]{:T(512)S(6)} %compare.3, bf16[40,128,102]{2,0,1:T(8,128)(2,1)} %get-tuple-element.336), kind=kOutput, calls=%fused_computation.19.clone.1 | convolution fusion | flops 1413021696 | bytes 6232576 | tf_op jit(solution)/shard_map/while/body/eval_jaxpr/bae,aei->bi/dot_general | solution.py:99
  109.9 0.7 dynamic-slice_bitcast_fusion.5
  110.6 2.2 %fusion.59 = f32[2048,32]{0,1:T(8,128)S(1)} fusion(f32[32,40]{1,0:T(8,128)S(1)} %dynamic-slice_bitcast_fusion.5, s32[32,40]{1,0:T(8,128)S(1)} %dynamic-slice_bitcast_fusion.4), kind=kLoop, calls=%fused_computation.15.clone.1 | loop fusion | flops 7798784 | bytes 272384 | tf_op jit(solution)/shard_map/while/body/eval_jaxpr/reduce_sum | solution.py:103
  112.8 2.3 %convolution_add_fusion.2 = f32[2048,256]{1,0:T(8,128)} fusion(f32[2048,256]{1,0:T(8,128)S(1)} %fusion.58, f32[2048,32]{0,1:T(8,128)S(1)} %fusion.59, bf16[128,256]{1,0:T(8,128)(2,1)S(1)} %get-tuple-element.339, s32[]{:T(128)S(6)} %select_n.26), kind=kOutput, calls=%fused_computation.18.clone.1 | convolution fusion | flops 201850880 | bytes 4472836 | tf_op jit(solution)/shard_map/while/body/eval_jaxpr/dot_general | solution.py:105
  116.3 0.7 dynamic-slice_bitcast_fusion.4
  117.1 5.4 %fusion.58 = f32[2048,256]{1,0:T(8,128)S(1)} fusion(s32[32,40]{1,0:T(8,128)S(1)} %dynamic-slice_bitcast_fusion.4, f32[2048,256]{1,0:T(8,128)} %get-tuple-element.321, bf16[102,128,256]{2,0,1:T(8,128)(2,1)} %get-tuple-element.337, s32[]{:T(128)S(6)} %select_n.26, pred[]{:T(512)S(6)} %compare.3, bf16[40,128,102]{2,0,1:T(8,128)(2,1)} %get-tuple-element.336), kind=kOutput, calls=%fused_computation.19.clone.1 | convolution fusion | flops 1413021696 | bytes 6232576 | tf_op jit(solution)/shard_map/while/body/eval_jaxpr/bae,aei->bi/dot_general | solution.py:99
  122.5 0.7 dynamic-slice_bitcast_fusion.5
  123.2 2.2 %fusion.59 = f32[2048,32]{0,1:T(8,128)S(1)} fusion(f32[32,40]{1,0:T(8,128)S(1)} %dynamic-slice_bitcast_fusion.5, s32[32,40]{1,0:T(8,128)S(1)} %dynamic-slice_bitcast_fusion.4), kind=kLoop, calls=%fused_computation.15.clone.1 | loop fusion | flops 7798784 | bytes 272384 | tf_op jit(solution)/shard_map/while/body/eval_jaxpr/reduce_sum | solution.py:103
  125.5 2.3 %convolution_add_fusion.2 = f32[2048,256]{1,0:T(8,128)} fusion(f32[2048,256]{1,0:T(8,128)S(1)} %fusion.58, f32[2048,32]{0,1:T(8,128)S(1)} %fusion.59, bf16[128,256]{1,0:T(8,128)(2,1)S(1)} %get-tuple-element.339, s32[]{:T(128)S(6)} %select_n.26), kind=kOutput, calls=%fused_computation.18.clone.1 | convolution fusion | flops 201850880 | bytes 4472836 | tf_op jit(solution)/shard_map/while/body/eval_jaxpr/dot_general | solution.py:105
  127.8 7.8 %all-to-all-start.1 = ((f32[16,128,256]{2,1,0:T(8,128)}), f32[16,128,256]{2,1,0:T(8,128)S(1)}, u32[]{:S(2)}, u32[]{:S(2)}) async-start(f32[16,128,256]{2,1,0:T(8,128)} %bitcast.68), calls=%async_computation.1 | async-start | bytes 4194304 | tf_op jit(solution)/shard_map/all_to_all | solution.py:32
  135.6 10.7 %fusion.39 = f32[1,128,256]{1,0,2:T(1,128)S(1)} fusion(f32[102,128,256]{1,0,2:T(8,128)} %bitcast.67, f32[102]{0:T(128)S(1)} %copy-done.2), kind=kOutput, calls=%fused_computation.44 | convolution fusion | flops 40108032 | bytes 13500824 | tf_op jit(solution)/shard_map/p,pai->ai/dot_general | solution.py:81
  146.4 22.6 %all-to-all-done.1 = f32[16,128,256]{2,1,0:T(8,128)S(1)} async-done(((f32[16,128,256]{2,1,0:T(8,128)}), f32[16,128,256]{2,1,0:T(8,128)S(1)}, u32[]{:S(2)}, u32[]{:S(2)}) %all-to-all-start.1) | async-done | bytes 2097184 | tf_op jit(solution)/shard_map/all_to_all | solution.py:32
  169.1 0.7 bitcast_add_fusion
  (20 shorter events, 1.2 us)
Async XLA Ops:
  0.0 70.3 %copy-start = (bf16[102,102]{1,0:T(8,128)(2,1)S(1)}, bf16[102,102]{1,0:T(8,128)(2,1)}, u32[]{:S(2)}) copy-start(bf16[102,102]{1,0:T(8,128)(2,1)} %param.15) | copy-start | bytes 62428
  0.0 16.3 %copy-start.2 = (f32[102]{0:T(128)S(1)}, f32[102]{0:T(128)}, u32[]{:S(2)}) copy-start(f32[102]{0:T(128)} %param.14) | copy-start | bytes 1228
  1.8 22.0 %all-to-all-start = ((bf16[8,128,256]{2,1,0:T(8,128)(2,1)}), bf16[8,128,256]{2,1,0:T(8,128)(2,1)S(1)}, u32[]{:S(2)}, u32[]{:S(2)}) async-start(bf16[8,128,256]{2,1,0:T(8,128)(2,1)} %broadcast_in_dim.38), calls=%async_computation | async-start | bytes 1048576 | tf_op jit(solution)/shard_map/all_to_all | solution.py:11
  16.3 10.5 %copy-start.1 = (s32[40,256]{1,0:T(8,128)S(1)}, s32[40,256]{1,0:T(8,128)}, u32[]{:S(2)}) copy-start(s32[40,256]{1,0:T(8,128)} %param.16) | copy-start | bytes 122884
  127.8 41.2 %all-to-all-start.1 = ((f32[16,128,256]{2,1,0:T(8,128)}), f32[16,128,256]{2,1,0:T(8,128)S(1)}, u32[]{:S(2)}, u32[]{:S(2)}) async-start(f32[16,128,256]{2,1,0:T(8,128)} %bitcast.68), calls=%async_computation.1 | async-start | bytes 4194304 | tf_op jit(solution)/shard_map/all_to_all | solution.py:32
where the time goes:
time: 171 us; the launch traced here: 170 us
  matrix products  76.6 us (45%)
  local copies, waits for them, and re-layouts  29.8 us (17%)
  other arithmetic  23.6 us (14%)
  waiting for transfers between devices  22.6 us (13%)
  starting transfers between devices  13.6 us (8%)
  loops' own time  3.63 us (2%)
    dot_general x2, matrix products, beta_block(): jnp.einsum('aei,eip->pai', picked, hot_cols, preferred_element_type=jnp.f...  27.8 us
    all_to_all x1, waiting for transfers between devices, summed_on_arrival(): lax.all_to_all(parts, axis, split_axis=0, concat_axis=0, tiled=True)  22.6 us
    dot_general x4, matrix products, accumulate(): jnp.einsum('bae,aei->bi', spread, lifted_bf, preferred_element_type=jnp.f...  21.1 us
    reshape x1, local copies, waits for them, and re-layouts, shards(): jnp.transpose(blocks, (1, 2, 0, 3))  12.9 us
    dot_general x1, matrix products, shards(): same_beta = jnp.einsum('p,pai->ai', one_body, density, precision=precise)  10.7 us
    dot_general x4, matrix products, accumulate(): jnp.dot(level_map, own_block, precision=precise)  9.38 us
    reduce_sum x4, other arithmetic, accumulate(): jnp.sum(jnp.where(matches, level_rows.T[None, :, :], jnp.float32(0.0)), a...  8.95 us
    all_to_all x1, starting transfers between devices, summed_on_arrival(): lax.all_to_all(parts, axis, split_axis=0, concat_axis=0, tiled=True)  7.77 us
  transfers between devices with their start and end apart: 2, of which 1 were waited for; matrix products, arithmetic and copies ran while one was open for 16% of the time, Pallas kernels for 0%

commit v1 on v0

v1 whole, which is shorter than its diff:
```python
import functools

import jax
import jax.numpy as jnp
from jax import lax
from jax.experimental import pallas as pl
from jax.experimental.pallas import tpu as pltpu
from jax.sharding import PartitionSpec as P

BF = jnp.bfloat16
F32 = jnp.float32
NT = (((1,), (1,)), ((), ()))
TN = (((0,), (0,)), ((), ()))
LANES = 128
WIDE = 512
PICK_UNROLL = 2
DENS_UNROLL = 8


def iota(shape, dim):
    return lax.broadcasted_iota(jnp.int32, shape, dim)


def compute_kernel(
    hi_lane,
    rows_ref,
    one_ref,
    pair_ref,
    bt_ref,
    bp_ref,
    bs_ref,
    at_ref,
    ap_ref,
    as_ref,
    partial_ref,
    same_ref,
    code_ref,
    turned_ref,
    group_ref,
    dens_ref,
    sv_ref,
    lift_ref,
    lift_bf_ref,
    hot_ref,
    wide_ref,
    picked_ref,
):
    blocks, rows, cols = rows_ref.shape
    excits = bt_ref.shape[0]
    slots = excits + 2
    per_group = LANES // slots
    groups = group_ref.shape[0]
    used_groups = -(-cols // per_group)
    me_beta = lax.axis_index("beta")

    code_ref[...] = jnp.zeros_like(code_ref)
    listed = bt_ref[...] + 2048 * bp_ref[...] + (1 << 18) * bs_ref[...]
    code_ref[0:excits, :] = listed.astype(F32)
    own = me_beta * cols + iota((8, cols), 1)
    extra = iota((8, cols), 0)
    own = jnp.where(extra < 2, own + 2048 * (hi_lane + extra) + (1 << 18), 0)
    code_ref[excits : excits + 8, :] = own.astype(F32)
    turned_ref[...] = jnp.zeros_like(turned_ref)
    turned_ref[0:cols, :] = code_ref[...].T
    grouped = turned_ref[pl.ds(0, groups, stride=per_group), :]
    for t in range(1, per_group):
        shifted = turned_ref[pl.ds(t, groups, stride=per_group), :]
        grouped = grouped + pltpu.roll(shifted, t * slots, 1)
    group_ref[...] = grouped.astype(jnp.int32)

    one_row = one_ref[...]
    one_hi = one_row.astype(BF).astype(F32)
    one_lo = one_row - one_hi
    one_two = jnp.concatenate([one_hi, one_lo, jnp.zeros((6, LANES), F32)], axis=0)
    one_cols = jnp.concatenate([one_two, jnp.zeros((LANES - 8, LANES), F32)], axis=0).T
    lane = iota((LANES, LANES), 1)
    table = pair_ref[...].astype(F32)
    table = jnp.where(lane == hi_lane, one_cols[:, 0:1], table)
    table = jnp.where(lane == hi_lane + 1, one_cols[:, 1:2], table)
    table = table.astype(BF)

    def sv_step(e, carry):
        which = ap_ref[pl.ds(e, 1), :]
        sign = (2 * as_ref[pl.ds(e, 1), :] - 1).astype(F32)
        hot = jnp.where(iota((LANES, rows), 0) == which, sign, 0.0).astype(BF)
        sv = lax.dot_general(hot, table, TN, preferred_element_type=F32)
        sv_ref[pl.ds(pl.multiple_of(e * rows, rows), rows), :] = sv
        return carry

    lax.fori_loop(0, excits, sv_step, 0, unroll=8)
    sv_ref[excits * rows :, :] = jnp.zeros(((48 - excits) * rows, LANES), F32)
    sv_ref[excits * rows : (excits + 1) * rows, :] = jnp.broadcast_to(one_hi, (rows, LANES))
    sv_ref[(excits + 1) * rows : (excits + 2) * rows, :] = jnp.broadcast_to(one_lo, (rows, LANES))

    wide = wide_ref.shape[1]
    parts = blocks * cols // wide
    joined = wide // cols
    for m in range(blocks):
        wide_ref[
            (m // joined) * rows : (m // joined + 1) * rows,
            (m % joined) * cols : (m % joined + 1) * cols,
        ] = rows_ref[m]
    lane_row = iota((1, LANES), 1)
    lane_slot = lane_row // slots

    def pick_step(step, carry):
        coded = [group_ref[pl.ds(2 * step + u, 1), :] for u in range(2)]
        code = jnp.concatenate(coded, axis=1)
        target = jnp.bitwise_and(code, 2047)
        low = jnp.bitwise_and(target, wide - 1)
        block = target // wide
        sign = (2 * lax.shift_right_logical(code, 18) - 1).astype(F32)
        pick = jnp.where(iota((wide, 2 * LANES), 0) == low, sign, 0.0).astype(BF)
        found = jnp.dot(wide_ref[...], pick, preferred_element_type=F32)
        picked = found[0:rows]
        for m in range(1, parts):
            picked = jnp.where(block == m, found[m * rows : (m + 1) * rows], picked)
        picked = picked.astype(BF)
        for u in range(2):
            picked_ref[2 * step + u] = picked[:, u * LANES : (u + 1) * LANES]
        return carry

    lax.fori_loop(0, used_groups // 2, pick_step, 0, unroll=PICK_UNROLL)

    def density_step(g, carry):
        code = group_ref[pl.ds(g, 1), :]
        pair = jnp.bitwise_and(lax.shift_right_logical(code, 11), 127)
        goal = jnp.where(lane_slot < per_group, lane_slot * LANES + pair, -1)
        spots = iota((per_group * LANES, LANES), 0) == goal
        hot = jnp.where(spots, 1.0, 0.0).astype(BF)
        dens = lax.dot_general(picked_ref[g], hot, NT, preferred_element_type=F32)
        for t in range(per_group):
            base = (per_group * g + t) * rows
            dens_ref[pl.ds(pl.multiple_of(base, rows), rows), :] = dens[
                :, t * LANES : (t + 1) * LANES
            ]
        return carry

    lax.fori_loop(0, used_groups, density_step, 0, unroll=DENS_UNROLL)

    def lift_step(a, carry):
        weights = sv_ref[pl.ds(a, 48, stride=rows), :].astype(BF)
        dens = dens_ref[pl.ds(a, cols, stride=rows), :].astype(BF)
        out = lax.dot_general(weights, dens, NT, preferred_element_type=F32)
        for half in range(2):
            lift_ref[half, pl.ds(a, 48, stride=rows), :] = out[:, half * LANES : (half + 1) * LANES]
        return carry

    lax.fori_loop(0, rows, lift_step, 0, unroll=8)
    for half in range(2):
        at_half = slice(half * LANES, (half + 1) * LANES)
        same_ref[:, at_half] = (
            lift_ref[half, excits * rows : (excits + 1) * rows, :]
            + lift_ref[half, (excits + 1) * rows : (excits + 2) * rows, :]
        )
        lift_bf_ref[:, at_half] = lift_ref[half, 0 : excits * rows, :].astype(BF)

    tall = hot_ref.shape[0]

    def spread_step(d, carry):
        def hot_step(e, inner):
            goal = at_ref[pl.ds(e, 1), :] - d * tall
            hot = jnp.where(iota((tall, rows), 0) == goal, 1.0, 0.0).astype(BF)
            hot_ref[:, pl.ds(pl.multiple_of(e * rows, rows), rows)] = hot
            return inner

        lax.fori_loop(0, excits, hot_step, 0)
        out = jnp.dot(hot_ref[...], lift_bf_ref[...], preferred_element_type=F32)
        partial_ref[pl.ds(pl.multiple_of(d * tall, tall), tall), :] = out.astype(BF)
        return carry

    lax.fori_loop(0, partial_ref.shape[0] // tall, spread_step, 0)


def local_part(rows_whole, one_body, pair_integrals, bt, bp, bs, at, ap, asg, total_alpha):
    blocks, rows, cols = rows_whole.shape
    pairs = one_body.shape[0]
    excits = bt.shape[0]
    one_row = jnp.pad(one_body, (0, LANES - pairs)).reshape(1, LANES)
    table = jnp.pad(pair_integrals, ((0, LANES - pairs), (0, LANES - pairs)))
    per_group = LANES // (excits + 2)
    used = -(-cols // per_group)
    groups = -(-used // 8) * 8
    vmem = pl.BlockSpec(memory_space=pltpu.VMEM)
    return pl.pallas_call(
        functools.partial(compute_kernel, pairs),
        out_shape=(
            jax.ShapeDtypeStruct((total_alpha, cols), BF),
            jax.ShapeDtypeStruct((rows, cols), F32),
        ),
        in_specs=[vmem] * 9,
        out_specs=(vmem, vmem),
        scratch_shapes=[
            pltpu.VMEM((LANES, cols), F32),
            pltpu.VMEM((groups * per_group, LANES), F32),
            pltpu.VMEM((groups, LANES), jnp.int32),
            pltpu.VMEM((groups * per_group * rows, LANES), F32),
            pltpu.VMEM((48 * rows, LANES), F32),
            pltpu.VMEM((2, 48 * rows, LANES), F32),
            pltpu.VMEM((excits * rows, cols), BF),
            pltpu.VMEM((512, excits * rows), BF),
            pltpu.VMEM((blocks * rows * cols // WIDE, WIDE), BF),
            pltpu.VMEM((groups, rows, LANES), BF),
        ],
        compiler_params=pltpu.CompilerParams(vmem_limit_bytes=56 * 2**20),
    )(rows_whole, one_row, table, bt, bp, bs, at, ap, asg)


def sent_to_all(value, axis):
    copies = jnp.broadcast_to(value, (lax.axis_size(axis), *value.shape))
    return lax.all_to_all(copies, axis, split_axis=0, concat_axis=0, tiled=True)


def shards(
    ci_vector,
    one_body,
    pair_integrals,
    beta_target,
    beta_pair,
    beta_sign,
    alpha_target,
    alpha_pair,
    alpha_sign,
):
    alpha_count, beta_count = ci_vector.shape
    alpha_devices = lax.axis_size("alpha")
    rows_whole = sent_to_all(ci_vector.astype(BF), "beta")
    partial, same_beta = local_part(
        rows_whole,
        one_body,
        pair_integrals,
        beta_target,
        beta_pair,
        beta_sign,
        alpha_target,
        alpha_pair,
        alpha_sign,
        alpha_count * alpha_devices,
    )
    partial = partial.reshape(alpha_devices, alpha_count, beta_count)
    arrived = lax.all_to_all(partial, "alpha", split_axis=0, concat_axis=0, tiled=True)
    return arrived.astype(F32).sum(axis=0) + same_beta


def solution(mesh):
    placed = (
        P("alpha", "beta"),
        P(),
        P(),
        P(None, "beta"),
        P(None, "beta"),
        P(None, "beta"),
        P(None, "alpha"),
        P(None, "alpha"),
        P(None, "alpha"),
    )
    return jax.shard_map(
        shards, mesh=mesh, in_specs=placed, out_specs=P("alpha", "beta"), check_vma=False
    )
```

time: 171 us -> 92.1 us (0.54)
  matrix products: 76.6 us -> 0 us
  Pallas kernels: 0 us -> 47.9 us
  local copies, waits for them, and re-layouts: 29.8 us -> 3.61 us
  blocking collectives: 0 us -> 23.8 us
  other arithmetic: 23.6 us -> 1.73 us
  waiting for transfers between devices: 22.6 us -> 8.27 us
  starting transfers between devices: 13.6 us -> 5.8 us
  loops' own time: 3.63 us -> 0 us
    dot_general x12 -> x0, matrix products: 76.6 us -> none  [the longest x2 27.8 us: beta_block(): jnp.einsum('aei,eip->pai', picked, hot_cols, preferred_element_type=jnp.f...]
    pallas_call x0 -> x1, Pallas kernels: none -> 47.9 us  [local_part(): pl.pallas_call(functools.partial(compute_kernel, pairs), out_shape=(jax.S...]
    all_to_all x0 -> x1, blocking collectives: none -> 23.8 us  [shards(): lax.all_to_all(partial, 'alpha', split_axis=0, concat_axis=0, tiled=True)]
    all_to_all x1 -> x0, waiting for transfers between devices: 22.6 us -> none  [summed_on_arrival(): lax.all_to_all(parts, axis, split_axis=0, concat_axis=0, tiled=True)]
    reshape x1, local copies, waits for them, and re-layouts: 12.9 us -> 0.58 us  [local_part(): one_row = jnp.pad(one_body, (0, LANES - pairs)).reshape(1, LANES)]
    reduce_sum x5 -> x1, other arithmetic: 9.08 us -> 0.14 us  [shards(): return arrived.astype(F32).sum(axis=0) + same_beta]
    all_to_all x1, waiting for transfers between devices: 0.01 us -> 8.27 us  [sent_to_all(): return lax.all_to_all(copies, axis, split_axis=0, concat_axis=0, tiled=True)]
    convert_element_type x3 -> x1, other arithmetic: 8.74 us -> 0.92 us  [shards(): rows_whole = sent_to_all(ci_vector.astype(BF), 'beta')]
  transfers between devices with their start and end apart: 2 -> 1, of which waited for: 1 -> 1; matrix products, arithmetic and copies ran while one was open for 16% -> 1% of each run, Pallas kernels for 0% -> 0%
where the time goes in v1:
time: 92.1 us; the launch traced here: 91.2 us
  Pallas kernels  47.9 us (52%)
  blocking collectives  23.8 us (26%)
  waiting for transfers between devices  8.27 us (9%)
  starting transfers between devices  5.8 us (6%)
  local copies, waits for them, and re-layouts  3.61 us (4%)
  other arithmetic  1.73 us (2%)
    pallas_call x1, Pallas kernels, local_part(): pl.pallas_call(functools.partial(compute_kernel, pairs), out_shape=(jax.S...  47.9 us
    all_to_all x1, blocking collectives, shards(): lax.all_to_all(partial, 'alpha', split_axis=0, concat_axis=0, tiled=True)  23.8 us
    all_to_all x1, waiting for transfers between devices, sent_to_all(): return lax.all_to_all(copies, axis, split_axis=0, concat_axis=0, tiled=True)  8.27 us
    all_to_all x1, starting transfers between devices, sent_to_all(): return lax.all_to_all(copies, axis, split_axis=0, concat_axis=0, tiled=True)  5.8 us
  transfers between devices with their start and end apart: 1, of which 1 were waited for; matrix products, arithmetic and copies ran while one was open for 1% of the time, Pallas kernels for 0%

profile of v1, /device:TPU:1, one launch (start us, length us, event | category | flops | bytes accessed | tf_op | source)
XLA Modules:
  0.0 91.2 jit_solution(1727987220831981783)
XLA Ops:
  0.0 0.0 copy-start.2
  0.0 0.0 copy-start.3
  0.0 0.9 %convert_element_type.10 = bf16[128,256]{1,0:T(8,128)(2,1)S(1)} convert(f32[128,256]{1,0:T(8,128)} %param.9) | non-fusion elementwise | flops 32768 | bytes 196608 | tf_op jit(solution)/shard_map/convert_element_type | solution.py:227
  0.9 0.8 broadcast_in_dim.3
  1.8 5.8 %all-to-all-start = ((bf16[8,128,256]{2,1,0:T(8,128)(2,1)}), bf16[8,128,256]{2,1,0:T(8,128)(2,1)S(1)}, u32[]{:S(2)}, u32[]{:S(2)}) async-start(bf16[8,128,256]{2,1,0:T(8,128)(2,1)} %broadcast_in_dim.3), calls=%async_computation | async-start | bytes 1048576 | tf_op jit(solution)/shard_map/all_to_all | solution.py:211
  7.6 0.0 copy-done.2
  7.6 0.6 pad.9.pair_ref
  8.2 0.0 copy-done.3
  8.2 0.6 pad_bitcast_fusion.one_ref
  8.8 8.3 %all-to-all-done.rows_ref = bf16[8,128,256]{2,1,0:T(8,128)(2,1)S(1)} async-done(((bf16[8,128,256]{2,1,0:T(8,128)(2,1)}), bf16[8,128,256]{2,1,0:T(8,128)(2,1)S(1)}, u32[]{:S(2)}, u32[]{:S(2)}) %all-to-all-start) | async-done | bytes 524320 | tf_op jit(solution)/shard_map/all_to_all | solution.py:211
  17.0 0.0 copy-start
  17.0 0.8 copy-done
  17.9 47.9 %shard_map.91 = (bf16[2048,256]{1,0:T(8,128)(2,1)}, f32[128,256]{1,0:T(8,128)}) custom-call(bf16[8,128,256]{2,1,0:T(8,128)(2,1)} %copy-done, f32[1,128]{1,0:T(1,128)} %pad_bitcast_fusion.one_ref, bf16[128,128]{1,0:T(8,128)(2,1)} %pad.9.pair_ref, s32[40,256]{1,0:T(8,128)} %bt_ref.1, s32[40,256]{1,0:T(8,128)} %bp_ref.1, s32[40,256]{1,0:T(8,128)} %bs_ref.1, ...), custom_call_target="tpu_custom_call" | custom-call | tf_op jit(solution)/shard_map/pallas_call | solution.py:185
  65.8 23.8 %all_to_all.10 = bf16[16,128,256]{2,1,0:T(8,128)(2,1)S(1)} all-to-all(bf16[16,128,256]{2,1,0:T(8,128)(2,1)} %bitcast.3), channel_id=1, replica_groups=mesh['alpha'=16,'beta'=8] {'alpha'}, dimensions={0} | all-to-all | bytes 2097152 | tf_op jit(solution)/shard_map/all_to_all | solution.py:241
  89.6 0.0 copy-start.1
  89.6 0.1 convert_reduce_fusion
  89.8 0.8 copy-done.1
  90.5 0.7 add.7
Async XLA Ops:
  0.0 7.6 %copy-start.2 = (bf16[102,102]{1,0:T(8,128)(2,1)S(1)}, bf16[102,102]{1,0:T(8,128)(2,1)}, u32[]{:S(2)}) copy-start(bf16[102,102]{1,0:T(8,128)(2,1)} %param.11) | copy-start | bytes 62428
  0.0 8.2 %copy-start.3 = (f32[102]{0:T(128)S(1)}, f32[102]{0:T(128)}, u32[]{:S(2)}) copy-start(f32[102]{0:T(128)} %param.10) | copy-start | bytes 1228
  1.8 15.3 %all-to-all-start = ((bf16[8,128,256]{2,1,0:T(8,128)(2,1)}), bf16[8,128,256]{2,1,0:T(8,128)(2,1)S(1)}, u32[]{:S(2)}, u32[]{:S(2)}) async-start(bf16[8,128,256]{2,1,0:T(8,128)(2,1)} %broadcast_in_dim.3), calls=%async_computation | async-start | bytes 1048576 | tf_op jit(solution)/shard_map/all_to_all | solution.py:211
  17.0 0.8 copy-start
  89.6 0.9 copy-start.1

commit v2 on v1

v2 whole, which is shorter than its diff:
```python
import functools

import jax
import jax.numpy as jnp
from jax import lax
from jax.experimental import pallas as pl
from jax.experimental.pallas import tpu as pltpu
from jax.sharding import PartitionSpec as P

BF = jnp.bfloat16
F32 = jnp.float32
MESH = pl.DeviceIdType.MESH
NT = (((1,), (1,)), ((), ()))
TN = (((0,), (0,)), ((), ()))
LANES = 128
WIDE = 512
DS = 132
SS = 136
LS = 136
PICK_UNROLL = 4
DENS_UNROLL = 8


def iota(shape, dim):
    return lax.broadcasted_iota(jnp.int32, shape, dim)


def compute_kernel(
    hi_lane,
    ci_ref,
    one_ref,
    pair_ref,
    bt_ref,
    bp_ref,
    bs_ref,
    at_ref,
    ap_ref,
    as_ref,
    out_ref,
    rows_ref,
    part_ref,
    arrive_ref,
    one_pad_ref,
    pair_pad_ref,
    code_ref,
    turned_ref,
    group_ref,
    dens_ref,
    sv_ref,
    lift_ref,
    lift_bf_ref,
    wide_ref,
    picked_ref,
    beta_send,
    beta_recv,
    alpha_send,
    alpha_recv,
):
    blocks, rows, cols = rows_ref.shape
    excits = bt_ref.shape[0]
    slots = excits + 2
    per_group = LANES // slots
    groups = group_ref.shape[0]
    used_groups = -(-cols // per_group)
    me_beta = lax.axis_index("beta")
    me_alpha = lax.axis_index("alpha")
    strings = arrive_ref.shape[0]

    barrier = pltpu.get_barrier_semaphore()
    for r in range(1, blocks):
        peer = {"beta": lax.rem(me_beta + r, blocks)}
        pl.semaphore_signal(barrier, inc=1, device_id=peer, device_id_type=MESH)
    for r in range(1, strings):
        peer = {"alpha": lax.rem(me_alpha + r, strings)}
        pl.semaphore_signal(barrier, inc=1, device_id=peer, device_id_type=MESH)
    rows_ref[me_beta] = ci_ref[...].astype(BF)
    pl.semaphore_wait(barrier, blocks + strings - 2)

    def row_copy(source, target):
        return pltpu.make_async_remote_copy(
            src_ref=rows_ref.at[source],
            dst_ref=rows_ref.at[source],
            send_sem=beta_send.at[target],
            recv_sem=beta_recv.at[source],
            device_id={"beta": target},
            device_id_type=MESH,
        )

    def part_copy(source, target):
        return pltpu.make_async_remote_copy(
            src_ref=part_ref.at[target],
            dst_ref=arrive_ref.at[source],
            send_sem=alpha_send.at[target],
            recv_sem=alpha_recv.at[source],
            device_id={"alpha": target},
            device_id_type=MESH,
        )

    for r in range(1, blocks):
        row_copy(me_beta, lax.rem(me_beta + r, blocks)).start()

    code_ref[...] = jnp.zeros_like(code_ref)
    listed = bt_ref[...] + 2048 * bp_ref[...] + (1 << 18) * bs_ref[...]
    code_ref[0:excits, :] = listed.astype(F32)
    own = me_beta * cols + iota((8, cols), 1)
    extra = iota((8, cols), 0)
    own = jnp.where(extra < 2, own + 2048 * (hi_lane + extra) + (1 << 18), 0)
    code_ref[excits : excits + 8, :] = own.astype(F32)
    turned_ref[...] = jnp.zeros_like(turned_ref)
    turned_ref[0:cols, :] = code_ref[...].T
    grouped = turned_ref[pl.ds(0, groups, stride=per_group), :]
    for t in range(1, per_group):
        shifted = turned_ref[pl.ds(t, groups, stride=per_group), :]
        grouped = grouped + pltpu.roll(shifted, t * slots, 1)
    group_ref[...] = grouped.astype(jnp.int32)

    pairs = pair_ref.shape[0]
    one_pad_ref[...] = jnp.zeros_like(one_pad_ref)
    one_pad_ref[0:1, 0:pairs] = one_ref[...]
    pair_pad_ref[...] = jnp.zeros_like(pair_pad_ref)
    pair_pad_ref[0:pairs, 0:pairs] = pair_ref[...].astype(F32)
    one_row = one_pad_ref[0:1, :]
    one_hi = one_row.astype(BF).astype(F32)
    one_lo = one_row - one_hi
    one_two = jnp.concatenate([one_hi, one_lo, jnp.zeros((6, LANES), F32)], axis=0)
    one_cols = jnp.concatenate([one_two, jnp.zeros((LANES - 8, LANES), F32)], axis=0).T
    lane = iota((LANES, LANES), 1)
    table = pair_pad_ref[...]
    table = jnp.where(lane == hi_lane, one_cols[:, 0:1], table)
    table = jnp.where(lane == hi_lane + 1, one_cols[:, 1:2], table)
    table = table.astype(BF)

    def sv_step(e, carry):
        which = ap_ref[pl.ds(e, 1), :]
        sign = (2 * as_ref[pl.ds(e, 1), :] - 1).astype(F32)
        hot = jnp.where(iota((LANES, rows), 0) == which, sign, 0.0).astype(BF)
        sv = lax.dot_general(hot, table, TN, preferred_element_type=F32)
        sv_ref[pl.ds(pl.multiple_of(e * SS, 8), rows), :] = sv
        return carry

    lax.fori_loop(0, excits, sv_step, 0, unroll=8)
    for e, row in enumerate((one_hi, one_lo)):
        start = (excits + e) * SS
        sv_ref[start : start + rows, :] = jnp.broadcast_to(row, (rows, LANES))
    sv_ref[(excits + 2) * SS :, :] = jnp.zeros(((46 - excits) * SS, LANES), F32)

    for r in range(1, blocks):
        row_copy(lax.rem(me_beta + r, blocks), me_beta).wait_recv()

    wide = wide_ref.shape[1]
    parts = blocks * cols // wide
    joined = wide // cols
    for m in range(blocks):
        wide_ref[
            (m // joined) * rows : (m // joined + 1) * rows,
            (m % joined) * cols : (m % joined + 1) * cols,
        ] = rows_ref[m]
    lane_row = iota((1, LANES), 1)
    lane_slot = lane_row // slots

    def pick_step(step, carry):
        coded = [group_ref[pl.ds(2 * step + u, 1), :] for u in range(2)]
        code = jnp.concatenate(coded, axis=1)
        target = jnp.bitwise_and(code, 2047)
        low = jnp.bitwise_and(target, wide - 1)
        block = target // wide
        sign = (2 * lax.shift_right_logical(code, 18) - 1).astype(F32)
        pick = jnp.where(iota((wide, 2 * LANES), 0) == low, sign, 0.0).astype(BF)
        found = jnp.dot(wide_ref[...], pick, preferred_element_type=F32)
        picked = found[0:rows]
        for m in range(1, parts):
            picked = jnp.where(block == m, found[m * rows : (m + 1) * rows], picked)
        picked = picked.astype(BF)
        for u in range(2):
            picked_ref[2 * step + u] = picked[:, u * LANES : (u + 1) * LANES]
        return carry

    lax.fori_loop(0, used_groups // 2, pick_step, 0, unroll=PICK_UNROLL)

    def density_step(g, carry):
        code = group_ref[pl.ds(g, 1), :]
        pair = jnp.bitwise_and(lax.shift_right_logical(code, 11), 127)
        goal = jnp.where(lane_slot < per_group, lane_slot * LANES + pair, -1)
        spots = iota((per_group * LANES, LANES), 0) == goal
        hot = jnp.where(spots, 1.0, 0.0).astype(BF)
        dens = lax.dot_general(picked_ref[g], hot, NT, preferred_element_type=F32)
        for t in range(per_group):
            base = (per_group * g + t) * DS
            dens_ref[pl.ds(pl.multiple_of(base, 4), rows), :] = dens[
                :, t * LANES : (t + 1) * LANES
            ]
        return carry

    lax.fori_loop(0, used_groups, density_step, 0, unroll=DENS_UNROLL)

    def lift_step(a, carry):
        weights = sv_ref[pl.ds(a, 48, stride=SS), :].astype(BF)
        dens = dens_ref[pl.ds(a, cols, stride=DS), :].astype(BF)
        out = lax.dot_general(weights, dens, NT, preferred_element_type=F32)
        for half in range(2):
            lift_ref[half, pl.ds(a, 48, stride=LS), :] = out[:, half * LANES : (half + 1) * LANES]
        return carry

    lax.fori_loop(0, rows, lift_step, 0, unroll=16)
    for half in range(2):
        at_half = slice(half * LANES, (half + 1) * LANES)
        for e in range(excits):
            lift_bf_ref[e * rows : (e + 1) * rows, at_half] = lift_ref[
                half, e * LS : e * LS + rows, :
            ].astype(BF)

    tall = 4 * rows
    mine, place = me_alpha // 4, lax.rem(me_alpha, 4)
    turns = strings // 4

    def spread_step(s, carry):
        group = lax.rem(mine + 1 + s, turns)
        hots = []
        for e in range(excits):
            goal = at_ref[e : e + 1, :] - group * tall
            hots.append(jnp.where(iota((tall, rows), 0) == goal, 1.0, 0.0).astype(BF))
        hot = jnp.concatenate(hots, axis=1)
        out = jnp.dot(hot, lift_bf_ref[...], preferred_element_type=F32)
        for t in range(4):
            part_ref[4 * group + t] = out[t * rows : (t + 1) * rows].astype(BF)
        for t in range(4):
            target = 4 * group + lax.rem(place + 1 + t, 4)

            @pl.when(target != me_alpha)
            def _():
                part_copy(me_alpha, target).start()

        return carry

    lax.fori_loop(0, turns, spread_step, 0)

    for half in range(2):
        at_half = slice(half * LANES, (half + 1) * LANES)
        out_ref[:, at_half] = (
            lift_ref[half, excits * LS : excits * LS + rows, :]
            + lift_ref[half, (excits + 1) * LS : (excits + 1) * LS + rows, :]
        )
    total = out_ref[...] + part_ref[me_alpha].astype(F32)
    for r in range(1, strings):
        source = lax.rem(me_alpha + strings - r, strings)
        part_copy(source, me_alpha).wait_recv()
        total = total + arrive_ref[source].astype(F32)
    out_ref[...] = total
    for r in range(1, blocks):
        row_copy(me_beta, lax.rem(me_beta + r, blocks)).wait_send()
    for r in range(1, strings):
        part_copy(me_alpha, lax.rem(me_alpha + r, strings)).wait_send()


def shards(ci_vector, one_body, pair_integrals, bt, bp, bs, at, ap, asg):
    rows, cols = ci_vector.shape
    blocks, strings = lax.axis_size("beta"), lax.axis_size("alpha")
    pairs = one_body.shape[0]
    excits = bt.shape[0]
    per_group = LANES // (excits + 2)
    used = -(-cols // per_group)
    groups = -(-used // 8) * 8
    vmem = pl.BlockSpec(memory_space=pltpu.VMEM)
    return pl.pallas_call(
        functools.partial(compute_kernel, pairs),
        out_shape=jax.ShapeDtypeStruct((rows, cols), F32),
        in_specs=[vmem] * 9,
        out_specs=vmem,
        scratch_shapes=[
            pltpu.VMEM((blocks, rows, cols), BF),
            pltpu.VMEM((strings, rows, cols), BF),
            pltpu.VMEM((strings, rows, cols), BF),
            pltpu.VMEM((8, LANES), F32),
            pltpu.VMEM((LANES, LANES), F32),
            pltpu.VMEM((LANES, cols), F32),
            pltpu.VMEM((groups * per_group, LANES), F32),
            pltpu.VMEM((groups, LANES), jnp.int32),
            pltpu.VMEM((groups * per_group * DS, LANES), F32),
            pltpu.VMEM((48 * SS, LANES), F32),
            pltpu.VMEM((2, 48 * LS, LANES), F32),
            pltpu.VMEM((excits * rows, cols), BF),
            pltpu.VMEM((blocks * rows * cols // WIDE, WIDE), BF),
            pltpu.VMEM((groups, rows, LANES), BF),
            pltpu.SemaphoreType.DMA((blocks,)),
            pltpu.SemaphoreType.DMA((blocks,)),
            pltpu.SemaphoreType.DMA((strings,)),
            pltpu.SemaphoreType.DMA((strings,)),
        ],
        compiler_params=pltpu.CompilerParams(
            vmem_limit_bytes=56 * 2**20, collective_id=0, has_side_effects=True
        ),
    )(ci_vector, one_body.reshape(1, pairs), pair_integrals, bt, bp, bs, at, ap, asg)


def solution(mesh):
    placed = (
        P("alpha", "beta"),
        P(),
        P(),
        P(None, "beta"),
        P(None, "beta"),
        P(None, "beta"),
        P(None, "alpha"),
        P(None, "alpha"),
        P(None, "alpha"),
    )
    return jax.shard_map(
        shards, mesh=mesh, in_specs=placed, out_specs=P("alpha", "beta"), check_vma=False
    )
```

time: 92.1 us -> 55.9 us (0.61)
  blocking collectives: 23.8 us -> 0 us
  waiting for transfers between devices: 8.27 us -> 0 us
  Pallas kernels: 47.9 us -> 54.1 us
  starting transfers between devices: 5.8 us -> 0 us
  local copies, waits for them, and re-layouts: 3.61 us -> 1.57 us
  other arithmetic: 1.73 us -> 0 us
    all_to_all x1 -> x0, blocking collectives: 23.8 us -> none  [shards(): lax.all_to_all(partial, 'alpha', split_axis=0, concat_axis=0, tiled=True)]
    all_to_all x1 -> x0, waiting for transfers between devices: 8.27 us -> none  [sent_to_all(): return lax.all_to_all(copies, axis, split_axis=0, concat_axis=0, tiled=True)]
    pallas_call x1, Pallas kernels: 47.9 us -> 54.1 us  [shards(): pl.pallas_call(functools.partial(compute_kernel, pairs), out_shape=jax.Sh...]
    all_to_all x1 -> x0, starting transfers between devices: 5.8 us -> none  [sent_to_all(): return lax.all_to_all(copies, axis, split_axis=0, concat_axis=0, tiled=True)]
  transfers between devices with their start and end apart: 1 -> 0, of which waited for: 1 -> 0; matrix products, arithmetic and copies ran while one was open for 1% -> 0% of each run, Pallas kernels for 0% -> 0%
where the time goes in v2:
time: 55.9 us; the launch traced here: 55.7 us
  Pallas kernels  54.1 us (97%)
  local copies, waits for them, and re-layouts  1.57 us (3%)
    pallas_call x1, Pallas kernels, shards(): pl.pallas_call(functools.partial(compute_kernel, pairs), out_shape=jax.Sh...  54.1 us
    unnamed x1, local copies, waits for them, and re-layouts  1.57 us

profile of v2, /device:TPU:1, one launch (start us, length us, event | category | flops | bytes accessed | tf_op | source)
XLA Modules:
  0.0 55.7 jit_solution(14557279100575754138)
XLA Ops:
  0.0 54.1 %shard_map.91 = f32[128,256]{1,0:T(8,128)} custom-call(f32[128,256]{1,0:T(8,128)} %ci_ref.1, f32[1,102]{1,0:T(1,128)} %bitcast.1, bf16[102,102]{1,0:T(8,128)(2,1)} %pair_ref.1, s32[40,256]{1,0:T(8,128)} %bt_ref.1, s32[40,256]{1,0:T(8,128)} %bp_ref.1, s32[40,256]{1,0:T(8,128)} %bs_ref.1, s32[40,128]{1,0:T(8,128)} %at_ref.1, s32[40,128]{1,0:T(8,128)} %ap_ref.1, ...), custom_call_target="tpu_custom_call" | custom-call | tf_op jit(solution)/shard_map/pallas_call | solution.py:264
  54.2 1.6 %copy.11 = f32[128,256]{1,0:T(8,128)} copy(f32[128,256]{1,0:T(8,128)} %shard_map.91) | data formatting | bytes 262144

commit v3 on v2

--- a/solution.py
+++ b/solution.py
@@ -38,8 +38,12 @@
     as_ref,
     out_ref,
     rows_ref,
-    part_ref,
-    arrive_ref,
+    near_part_ref,
+    far_part_ref,
+    near_got_ref,
+    far_got_ref,
+    last_part_ref,
+    last_got_ref,
     one_pad_ref,
     pair_pad_ref,
     code_ref,
@@ -51,10 +55,15 @@
     lift_bf_ref,
     wide_ref,
     picked_ref,
+    order_ref,
     beta_send,
     beta_recv,
-    alpha_send,
-    alpha_recv,
+    near_send,
+    near_recv,
+    far_send,
+    far_recv,
+    last_send,
+    last_recv,
 ):
     blocks, rows, cols = rows_ref.shape
     excits = bt_ref.shape[0]
@@ -64,40 +73,108 @@
     used_groups = -(-cols // per_group)
     me_beta = lax.axis_index("beta")
     me_alpha = lax.axis_index("alpha")
-    strings = arrive_ref.shape[0]
 
     barrier = pltpu.get_barrier_semaphore()
-    for r in range(1, blocks):
-        peer = {"beta": lax.rem(me_beta + r, blocks)}
-        pl.semaphore_signal(barrier, inc=1, device_id=peer, device_id_type=MESH)
-    for r in range(1, strings):
-        peer = {"alpha": lax.rem(me_alpha + r, strings)}
-        pl.semaphore_signal(barrier, inc=1, device_id=peer, device_id_type=MESH)
+    chips = blocks // 2
+    here, core = me_beta // 2, lax.rem(me_beta, 2)
+    sibling = 2 * here + 1 - core
+    right = 2 * lax.rem(here + 1, chips) + core
+    left = 2 * lax.rem(here + chips - 1, chips) + core
+    across = 2 * lax.rem(here + 2, chips) + core
+    beta_peers = (sibling, left, right, across)
+    for peer in beta_peers:
+        pl.semaphore_signal(barrier, inc=1, device_id={"beta": peer}, device_id_type=MESH)
+    mine, place = me_alpha // 4, lax.rem(me_alpha, 4)
+
+    def at_far(far):
+        return {"alpha": 4 * far + place}
+
+    def at_near(near):
+        return {"alpha": 4 * mine + near}
+
+    def turned(start, r):
+        return lax.rem(start + r, 4)
+
+    for r in range(1, 4):
+        for peer in (at_far(turned(mine, r)), at_near(turned(place, r))):
+            pl.semaphore_signal(barrier, inc=1, device_id=peer, device_id_type=MESH)
     rows_ref[me_beta] = ci_ref[...].astype(BF)
-    pl.semaphore_wait(barrier, blocks + strings - 2)
-
-    def row_copy(source, target):
+    pl.semaphore_wait(barrier, len(beta_peers) + 6)
+
+    def row_copy(k, block, target):
         return pltpu.make_async_remote_copy(
-            src_ref=rows_ref.at[source],
-            dst_ref=rows_ref.at[source],
-            send_sem=beta_send.at[target],
-            recv_sem=beta_recv.at[source],
+            src_ref=rows_ref.at[block],
+            dst_ref=rows_ref.at[block],
+            send_sem=beta_send.at[k],
+            recv_sem=beta_recv.at[k],
             device_id={"beta": target},
             device_id_type=MESH,
         )
 
-    def part_copy(source, target):
+    def other(block):
+        return block + 1 - 2 * core
+
+    sends = [
+        row_copy(0, me_beta, across),
+        row_copy(1, me_beta, right),
+        row_copy(2, me_beta, left),
+        row_copy(3, me_beta, sibling),
+        row_copy(4, across, sibling),
+        row_copy(5, left, sibling),
+        row_copy(6, right, sibling),
+    ]
+    arrivals = [
+        row_copy(0, across, me_beta),
+        row_copy(1, left, me_beta),
+        row_copy(2, right, me_beta),
+        row_copy(3, sibling, me_beta),
+        row_copy(4, other(across), me_beta),
+        row_copy(5, other(left), me_beta),
+        row_copy(6, other(right), me_beta),
+    ]
+
+    def near_copy(source, target):
         return pltpu.make_async_remote_copy(
-            src_ref=part_ref.at[target],
-            dst_ref=arrive_ref.at[source],
-            send_sem=alpha_send.at[target],
-            recv_sem=alpha_recv.at[source],
-            device_id={"alpha": target},
+            src_ref=near_part_ref.at[target],
+            dst_ref=near_got_ref.at[source],
+            send_sem=near_send.at[target],
+            recv_sem=near_recv.at[source],
+            device_id=at_near(target),
             device_id_type=MESH,
         )
 
-    for r in range(1, blocks):
-        row_copy(me_beta, lax.rem(me_beta + r, blocks)).start()
+    def far_copy(source, target, near):
+        return pltpu.make_async_remote_copy(
+            src_ref=far_part_ref.at[near, target],
+            dst_ref=far_got_ref.at[source, near],
+            send_sem=far_send.at[near, target],
+            recv_sem=far_recv.at[source, near],
+            device_id=at_far(target),
+            device_id_type=MESH,
+        )
+
+    def near_last(source, target):
+        return pltpu.make_async_remote_copy(
+            src_ref=last_part_ref.at[1, target],
+            dst_ref=last_got_ref.at[1, source],
+            send_sem=last_send.at[1, target],
+            recv_sem=last_recv.at[1, source],
+            device_id=at_near(target),
+            device_id_type=MESH,
+        )
+
+    def far_last(source, target):
+        return pltpu.make_async_remote_copy(
+            src_ref=last_part_ref.at[0, target],
+            dst_ref=last_got_ref.at[0, source],
+            send_sem=last_send.at[0, target],
+            recv_sem=last_recv.at[0, source],
+            device_id=at_far(target),
+            device_id_type=MESH,
+        )
+
+    for k in range(4):
+        sends[k].start()
 
     code_ref[...] = jnp.zeros_like(code_ref)
     listed = bt_ref[...] + 2048 * bp_ref[...] + (1 << 18) * bs_ref[...]
@@ -113,6 +190,10 @@
         shifted = turned_ref[pl.ds(t, groups, stride=per_group), :]
         grouped = grouped + pltpu.roll(shifted, t * slots, 1)
     group_ref[...] = grouped.astype(jnp.int32)
+
+    device = at_ref[...] // rows
+    near = jnp.bitwise_and(jnp.bitwise_and(device, 3) - place + 3, 3)
+    order_ref[...] = (4 * near + device // 4) * rows + jnp.bitwise_and(at_ref[...], rows - 1)
 
     pairs = pair_ref.shape[0]
     one_pad_ref[...] = jnp.zeros_like(one_pad_ref)
@@ -144,8 +225,11 @@
         sv_ref[start : start + rows, :] = jnp.broadcast_to(row, (rows, LANES))
     sv_ref[(excits + 2) * SS :, :] = jnp.zeros(((46 - excits) * SS, LANES), F32)
 
-    for r in range(1, blocks):
-        row_copy(lax.rem(me_beta + r, blocks), me_beta).wait_recv()
+    for k, passed in ((1, 5), (2, 6), (0, 4)):
+        arrivals[k].wait_recv()
+        sends[passed].start()
+    for k in (3, 5, 6, 4):
+        arrivals[k].wait_recv()
 
     wide = wide_ref.shape[1]
     parts = blocks * cols // wide
@@ -210,29 +294,29 @@
             ].astype(BF)
 
     tall = 4 * rows
-    mine, place = me_alpha // 4, lax.rem(me_alpha, 4)
-    turns = strings // 4
 
     def spread_step(s, carry):
-        group = lax.rem(mine + 1 + s, turns)
         hots = []
         for e in range(excits):
-            goal = at_ref[e : e + 1, :] - group * tall
+            goal = order_ref[e : e + 1, :] - s * tall
             hots.append(jnp.where(iota((tall, rows), 0) == goal, 1.0, 0.0).astype(BF))
         hot = jnp.concatenate(hots, axis=1)
-        out = jnp.dot(hot, lift_bf_ref[...], preferred_element_type=F32)
-        for t in range(4):
-            part_ref[4 * group + t] = out[t * rows : (t + 1) * rows].astype(BF)
-        for t in range(4):
-            target = 4 * group + lax.rem(place + 1 + t, 4)
-
-            @pl.when(target != me_alpha)
-            def _():
-                part_copy(me_alpha, target).start()
-
+        out = jnp.dot(hot, lift_bf_ref[...], preferred_element_type=F32).astype(BF)
+        near = turned(place, s + 1)
+        for far in range(4):
+            at_rows = slice(far * rows, (far + 1) * rows)
+            near_part_ref[near, far] = out[at_rows, 0:LANES]
+            far_part_ref[near, far] = out[at_rows, LANES : 2 * LANES]
+
+        @pl.when(s < 3)
+        def _():
+            near_copy(place, near).start()
+
+        for r in (2, 1, 3):
+            far_copy(mine, turned(mine, r), near).start()
         return carry
 
-    lax.fori_loop(0, turns, spread_step, 0)
+    lax.fori_loop(0, 4, spread_step, 0)
 
     for half in range(2):
         at_half = slice(half * LANES, (half + 1) * LANES)
@@ -240,21 +324,57 @@
             lift_ref[half, excits * LS : excits * LS + rows, :]
             + lift_ref[half, (excits + 1) * LS : (excits + 1) * LS + rows, :]
         )
-    total = out_ref[...] + part_ref[me_alpha].astype(F32)
-    for r in range(1, strings):
-        source = lax.rem(me_alpha + strings - r, strings)
-        part_copy(source, me_alpha).wait_recv()
-        total = total + arrive_ref[source].astype(F32)
-    out_ref[...] = total
-    for r in range(1, blocks):
-        row_copy(me_beta, lax.rem(me_beta + r, blocks)).wait_send()
-    for r in range(1, strings):
-        part_copy(me_alpha, lax.rem(me_alpha + r, strings)).wait_send()
+
+    for r in range(1, 4):
+        near_copy(turned(place, r), place).wait_recv()
+    for r in (2, 1, 3, 0):
+        far = turned(mine, r)
+        total = near_part_ref[place, far].astype(F32)
+        for q in range(1, 4):
+            total = total + near_got_ref[turned(place, q), far].astype(F32)
+        if r:
+            last_part_ref[0, far] = total.astype(BF)
+            far_last(mine, far).start()
+        else:
+            out_ref[:, 0:LANES] = out_ref[:, 0:LANES] + total
+
+    for r in (2, 1, 3, 0):
+        near = turned(place, r)
+        total = far_part_ref[near, mine].astype(F32)
+        for q in range(1, 4):
+            source = turned(mine, q)
+            far_copy(source, mine, near).wait_recv()
+            total = total + far_got_ref[source, near].astype(F32)
+        if r:
+            last_part_ref[1, near] = total.astype(BF)
+            near_last(place, near).start()
+        else:
+            out_ref[:, LANES : 2 * LANES] = out_ref[:, LANES : 2 * LANES] + total
+
+    total = out_ref[:, 0:LANES]
+    for r in range(1, 4):
+        far_last(turned(mine, r), mine).wait_recv()
+        total = total + last_got_ref[0, turned(mine, r)].astype(F32)
+    out_ref[:, 0:LANES] = total
+    total = out_ref[:, LANES : 2 * LANES]
+    for r in range(1, 4):
+        near_last(turned(place, r), place).wait_recv()
+        total = total + last_got_ref[1, turned(place, r)].astype(F32)
+    out_ref[:, LANES : 2 * LANES] = total
+
+    for copy in sends:
+        copy.wait_send()
+    for r in range(1, 4):
+        near_copy(place, turned(place, r)).wait_send()
+        far_last(mine, turned(mine, r)).wait_send()
+        near_last(place, turned(place, r)).wait_send()
+        for near in range(4):
+            far_copy(mine, turned(mine, r), near).wait_send()
 
 
 def shards(ci_vector, one_body, pair_integrals, bt, bp, bs, at, ap, asg):
     rows, cols = ci_vector.shape
-    blocks, strings = lax.axis_size("beta"), lax.axis_size("alpha")
+    blocks = lax.axis_size("beta")
     pairs = one_body.shape[0]
     excits = bt.shape[0]
     per_group = LANES // (excits + 2)
@@ -268,8 +388,12 @@
         out_specs=vmem,
         scratch_shapes=[
             pltpu.VMEM((blocks, rows, cols), BF),
-            pltpu.VMEM((strings, rows, cols), BF),
-            pltpu.VMEM((strings, rows, cols), BF),
+            pltpu.VMEM((4, 4, rows, LANES), BF),
+            pltpu.VMEM((4, 4, rows, LANES), BF),
+            pltpu.VMEM((4, 4, rows, LANES), BF),
+            pltpu.VMEM((4, 4, rows, LANES), BF),
+            pltpu.VMEM((2, 4, rows, LANES), BF),
+            pltpu.VMEM((2, 4, rows, LANES), BF),
             pltpu.VMEM((8, LANES), F32),
             pltpu.VMEM((LANES, LANES), F32),
             pltpu.VMEM((LANES, cols), F32),
@@ -281,10 +405,15 @@
             pltpu.VMEM((excits * rows, cols), BF),
             pltpu.VMEM((blocks * rows * cols // WIDE, WIDE), BF),
             pltpu.VMEM((groups, rows, LANES), BF),
+            pltpu.VMEM((excits, rows), jnp.int32),
             pltpu.SemaphoreType.DMA((blocks,)),
             pltpu.SemaphoreType.DMA((blocks,)),
-            pltpu.SemaphoreType.DMA((strings,)),
-            pltpu.SemaphoreType.DMA((strings,)),
+            pltpu.SemaphoreType.DMA((4,)),
+            pltpu.SemaphoreType.DMA((4,)),
+            pltpu.SemaphoreType.DMA((4, 4)),
+            pltpu.SemaphoreType.DMA((4, 4)),
+            pltpu.SemaphoreType.DMA((2, 4)),
+            pltpu.SemaphoreType.DMA((2, 4)),
         ],
         compiler_params=pltpu.CompilerParams(
             vmem_limit_bytes=56 * 2**20, collective_id=0, has_side_effects=True

time: 55.9 us -> 50.5 us (0.903)
  Pallas kernels: 54.1 us -> 48.8 us
    pallas_call x1, Pallas kernels: 54.1 us -> 48.8 us  [shards(): pl.pallas_call(functools.partial(compute_kernel, pairs), out_shape=jax.Sh...]
where the time goes in v3:
time: 50.5 us; the launch traced here: 50.4 us
  Pallas kernels  48.8 us (97%)
  local copies, waits for them, and re-layouts  1.57 us (3%)
    pallas_call x1, Pallas kernels, shards(): pl.pallas_call(functools.partial(compute_kernel, pairs), out_shape=jax.Sh...  48.8 us
    unnamed x1, local copies, waits for them, and re-layouts  1.57 us

profile of v3, /device:TPU:1, one launch (start us, length us, event | category | flops | bytes accessed | tf_op | source)
XLA Modules:
  0.0 50.4 jit_solution(6479631402397885247)
XLA Ops:
  0.0 48.8 %shard_map.91 = f32[128,256]{1,0:T(8,128)} custom-call(f32[128,256]{1,0:T(8,128)} %ci_ref.1, f32[1,102]{1,0:T(1,128)} %bitcast.1, bf16[102,102]{1,0:T(8,128)(2,1)} %pair_ref.1, s32[40,256]{1,0:T(8,128)} %bt_ref.1, s32[40,256]{1,0:T(8,128)} %bp_ref.1, s32[40,256]{1,0:T(8,128)} %bs_ref.1, s32[40,128]{1,0:T(8,128)} %at_ref.1, s32[40,128]{1,0:T(8,128)} %ap_ref.1, ...), custom_call_target="tpu_custom_call" | custom-call | tf_op jit(solution)/shard_map/pallas_call | solution.py:384
  48.8 1.6 %copy.11 = f32[128,256]{1,0:T(8,128)} copy(f32[128,256]{1,0:T(8,128)} %shard_map.91) | data formatting | bytes 262144

commit v4 on v3

--- a/solution.py
+++ b/solution.py
@@ -17,8 +17,7 @@
 DS = 132
 SS = 136
 LS = 136
-PICK_UNROLL = 4
-DENS_UNROLL = 8
+BATCH = 4
 
 
 def iota(shape, dim):
@@ -54,7 +53,8 @@
     lift_ref,
     lift_bf_ref,
     wide_ref,
-    picked_ref,
+    even_ref,
+    odd_ref,
     order_ref,
     beta_send,
     beta_recv,
@@ -70,7 +70,6 @@
     slots = excits + 2
     per_group = LANES // slots
     groups = group_ref.shape[0]
-    used_groups = -(-cols // per_group)
     me_beta = lax.axis_index("beta")
     me_alpha = lax.axis_index("alpha")
 
@@ -242,7 +241,7 @@
     lane_row = iota((1, LANES), 1)
     lane_slot = lane_row // slots
 
-    def pick_step(step, carry):
+    def pick_step(step, held, slot):
         coded = [group_ref[pl.ds(2 * step + u, 1), :] for u in range(2)]
         code = jnp.concatenate(coded, axis=1)
         target = jnp.bitwise_and(code, 2047)
@@ -256,26 +255,43 @@
             picked = jnp.where(block == m, found[m * rows : (m + 1) * rows], picked)
         picked = picked.astype(BF)
         for u in range(2):
-            picked_ref[2 * step + u] = picked[:, u * LANES : (u + 1) * LANES]
-        return carry
-
-    lax.fori_loop(0, used_groups // 2, pick_step, 0, unroll=PICK_UNROLL)
-
-    def density_step(g, carry):
+            held[2 * slot + u] = picked[:, u * LANES : (u + 1) * LANES]
+
+
+    def density_step(g, held, slot):
         code = group_ref[pl.ds(g, 1), :]
         pair = jnp.bitwise_and(lax.shift_right_logical(code, 11), 127)
         goal = jnp.where(lane_slot < per_group, lane_slot * LANES + pair, -1)
         spots = iota((per_group * LANES, LANES), 0) == goal
         hot = jnp.where(spots, 1.0, 0.0).astype(BF)
-        dens = lax.dot_general(picked_ref[g], hot, NT, preferred_element_type=F32)
+        dens = lax.dot_general(held[slot], hot, NT, preferred_element_type=F32)
         for t in range(per_group):
             base = (per_group * g + t) * DS
             dens_ref[pl.ds(pl.multiple_of(base, 4), rows), :] = dens[
                 :, t * LANES : (t + 1) * LANES
             ]
+
+    def both(j, last, held):
+        for u in range(BATCH):
+            if held is not None:
+                pick_step(BATCH * j + u, held, u)
+            if last is not None:
+                for v in (2 * u, 2 * u + 1):
+                    density_step(2 * BATCH * (j - 1) + v, last, v)
+
+    def both_step(k, carry):
+        both(2 * k + 1, even_ref, odd_ref)
+        both(2 * k + 2, odd_ref, even_ref)
         return carry
 
-    lax.fori_loop(0, used_groups, density_step, 0, unroll=DENS_UNROLL)
+    batches = groups // (2 * BATCH)
+    both(0, None, even_ref)
+    lax.fori_loop(0, (batches - 1) // 2, both_step, 0)
+    if batches % 2:
+        both(batches, even_ref, None)
+    else:
+        both(batches - 1, even_ref, odd_ref)
+        both(batches, odd_ref, None)
 
     def lift_step(a, carry):
         weights = sv_ref[pl.ds(a, 48, stride=SS), :].astype(BF)
@@ -379,7 +395,7 @@
     excits = bt.shape[0]
     per_group = LANES // (excits + 2)
     used = -(-cols // per_group)
-    groups = -(-used // 8) * 8
+    groups = -(-used // (2 * BATCH)) * 2 * BATCH
     vmem = pl.BlockSpec(memory_space=pltpu.VMEM)
     return pl.pallas_call(
         functools.partial(compute_kernel, pairs),
@@ -404,7 +420,8 @@
             pltpu.VMEM((2, 48 * LS, LANES), F32),
             pltpu.VMEM((excits * rows, cols), BF),
             pltpu.VMEM((blocks * rows * cols // WIDE, WIDE), BF),
-            pltpu.VMEM((groups, rows, LANES), BF),
+            pltpu.VMEM((2 * BATCH, rows, LANES), BF),
+            pltpu.VMEM((2 * BATCH, rows, LANES), BF),
             pltpu.VMEM((excits, rows), jnp.int32),
             pltpu.SemaphoreType.DMA((blocks,)),
             pltpu.SemaphoreType.DMA((blocks,)),

time: 50.5 us -> 46.7 us (0.925)
  Pallas kernels: 48.8 us -> 45 us
    pallas_call x1, Pallas kernels: 48.8 us -> 45 us  [shards(): pl.pallas_call(functools.partial(compute_kernel, pairs), out_shape=jax.Sh...]
where the time goes in v4:
time: 46.7 us; the launch traced here: 46.6 us
  Pallas kernels  45 us (96%)
  local copies, waits for them, and re-layouts  1.57 us (3%)
    pallas_call x1, Pallas kernels, shards(): pl.pallas_call(functools.partial(compute_kernel, pairs), out_shape=jax.Sh...  45 us
    unnamed x1, local copies, waits for them, and re-layouts  1.57 us

profile of v4, /device:TPU:1, one launch (start us, length us, event | category | flops | bytes accessed | tf_op | source)
XLA Modules:
  0.0 46.6 jit_solution(170078073822074064)
XLA Ops:
  0.0 45.0 %shard_map.91 = f32[128,256]{1,0:T(8,128)} custom-call(f32[128,256]{1,0:T(8,128)} %ci_ref.1, f32[1,102]{1,0:T(1,128)} %bitcast.1, bf16[102,102]{1,0:T(8,128)(2,1)} %pair_ref.1, s32[40,256]{1,0:T(8,128)} %bt_ref.1, s32[40,256]{1,0:T(8,128)} %bp_ref.1, s32[40,256]{1,0:T(8,128)} %bs_ref.1, s32[40,128]{1,0:T(8,128)} %at_ref.1, s32[40,128]{1,0:T(8,128)} %ap_ref.1, ...), custom_call_target="tpu_custom_call" | custom-call | tf_op jit(solution)/shard_map/pallas_call | solution.py:400
  45.0 1.6 %copy.11 = f32[128,256]{1,0:T(8,128)} copy(f32[128,256]{1,0:T(8,128)} %shard_map.91) | data formatting | bytes 262144

commit v5 on v4

--- a/solution.py
+++ b/solution.py
@@ -53,6 +53,7 @@
     lift_ref,
     lift_bf_ref,
     wide_ref,
+    own_ref,
     even_ref,
     odd_ref,
     order_ref,
@@ -194,6 +195,37 @@
     near = jnp.bitwise_and(jnp.bitwise_and(device, 3) - place + 3, 3)
     order_ref[...] = (4 * near + device // 4) * rows + jnp.bitwise_and(at_ref[...], rows - 1)
 
+    wide = wide_ref.shape[1]
+    arrivals[3].wait_recv()
+
+    def widen(r):
+        chip = 2 * turned(here, r)
+        for c in range(2):
+            wide_ref[r * rows : (r + 1) * rows, c * cols : (c + 1) * cols] = rows_ref[chip + c]
+
+    def pick_code(step):
+        coded = [group_ref[pl.ds(2 * step + u, 1), :] for u in range(2)]
+        code = jnp.concatenate(coded, axis=1)
+        target = jnp.bitwise_and(code, 2047)
+        low = jnp.bitwise_and(target, wide - 1)
+        sign = (2 * lax.shift_right_logical(code, 18) - 1).astype(F32)
+        pick = jnp.where(iota((wide, 2 * LANES), 0) == low, sign, 0.0).astype(BF)
+        return jnp.bitwise_and(target // wide - here + chips, chips - 1), pick
+
+    def own_step(step, carry):
+        unused, pick = pick_code(step)
+        found = jnp.dot(wide_ref[0:rows, :], pick, preferred_element_type=F32).astype(BF)
+        for u in range(2):
+            own_ref[2 * step + u] = found[:, u * LANES : (u + 1) * LANES]
+        return carry
+
+    widen(0)
+    lax.fori_loop(0, groups // 2, own_step, 0, unroll=4)
+
+    for k, passed in ((1, 5), (2, 6), (0, 4)):
+        arrivals[k].wait_recv()
+        sends[passed].start()
+
     pairs = pair_ref.shape[0]
     one_pad_ref[...] = jnp.zeros_like(one_pad_ref)
     one_pad_ref[0:1, 0:pairs] = one_ref[...]
@@ -224,39 +256,23 @@
         sv_ref[start : start + rows, :] = jnp.broadcast_to(row, (rows, LANES))
     sv_ref[(excits + 2) * SS :, :] = jnp.zeros(((46 - excits) * SS, LANES), F32)
 
-    for k, passed in ((1, 5), (2, 6), (0, 4)):
+    for k in (5, 6, 4):
         arrivals[k].wait_recv()
-        sends[passed].start()
-    for k in (3, 5, 6, 4):
-        arrivals[k].wait_recv()
-
-    wide = wide_ref.shape[1]
-    parts = blocks * cols // wide
-    joined = wide // cols
-    for m in range(blocks):
-        wide_ref[
-            (m // joined) * rows : (m // joined + 1) * rows,
-            (m % joined) * cols : (m % joined + 1) * cols,
-        ] = rows_ref[m]
+
+    for r in range(1, chips):
+        widen(r)
     lane_row = iota((1, LANES), 1)
     lane_slot = lane_row // slots
 
     def pick_step(step, held, slot):
-        coded = [group_ref[pl.ds(2 * step + u, 1), :] for u in range(2)]
-        code = jnp.concatenate(coded, axis=1)
-        target = jnp.bitwise_and(code, 2047)
-        low = jnp.bitwise_and(target, wide - 1)
-        block = target // wide
-        sign = (2 * lax.shift_right_logical(code, 18) - 1).astype(F32)
-        pick = jnp.where(iota((wide, 2 * LANES), 0) == low, sign, 0.0).astype(BF)
-        found = jnp.dot(wide_ref[...], pick, preferred_element_type=F32)
-        picked = found[0:rows]
-        for m in range(1, parts):
-            picked = jnp.where(block == m, found[m * rows : (m + 1) * rows], picked)
+        block, pick = pick_code(step)
+        found = jnp.dot(wide_ref[rows:, :], pick, preferred_element_type=F32)
+        picked = jnp.concatenate([own_ref[2 * step + u] for u in range(2)], axis=1).astype(F32)
+        for r in range(1, chips):
+            picked = jnp.where(block == r, found[(r - 1) * rows : r * rows], picked)
         picked = picked.astype(BF)
         for u in range(2):
             held[2 * slot + u] = picked[:, u * LANES : (u + 1) * LANES]
-
 
     def density_step(g, held, slot):
         code = group_ref[pl.ds(g, 1), :]
@@ -420,6 +436,7 @@
             pltpu.VMEM((2, 48 * LS, LANES), F32),
             pltpu.VMEM((excits * rows, cols), BF),
             pltpu.VMEM((blocks * rows * cols // WIDE, WIDE), BF),
+            pltpu.VMEM((groups, rows, LANES), BF),
             pltpu.VMEM((2 * BATCH, rows, LANES), BF),
             pltpu.VMEM((2 * BATCH, rows, LANES), BF),
             pltpu.VMEM((excits, rows), jnp.int32),

time: 46.7 us -> 45.1 us (0.966)
  Pallas kernels: 45 us -> 43.4 us
    pallas_call x1, Pallas kernels: 45 us -> 43.4 us  [shards(): pl.pallas_call(functools.partial(compute_kernel, pairs), out_shape=jax.Sh...]
where the time goes in v5:
time: 45.1 us; the launch traced here: 44.9 us
  Pallas kernels  43.4 us (96%)
  local copies, waits for them, and re-layouts  1.57 us (3%)
    pallas_call x1, Pallas kernels, shards(): pl.pallas_call(functools.partial(compute_kernel, pairs), out_shape=jax.Sh...  43.4 us
    unnamed x1, local copies, waits for them, and re-layouts  1.57 us

profile of v5, /device:TPU:1, one launch (start us, length us, event | category | flops | bytes accessed | tf_op | source)
XLA Modules:
  0.0 44.9 jit_solution(10805955056567865143)
XLA Ops:
  0.0 43.4 %shard_map.91 = f32[128,256]{1,0:T(8,128)} custom-call(f32[128,256]{1,0:T(8,128)} %ci_ref.1, f32[1,102]{1,0:T(1,128)} %bitcast.1, bf16[102,102]{1,0:T(8,128)(2,1)} %pair_ref.1, s32[40,256]{1,0:T(8,128)} %bt_ref.1, s32[40,256]{1,0:T(8,128)} %bp_ref.1, s32[40,256]{1,0:T(8,128)} %bs_ref.1, s32[40,128]{1,0:T(8,128)} %at_ref.1, s32[40,128]{1,0:T(8,128)} %ap_ref.1, ...), custom_call_target="tpu_custom_call" | custom-call | tf_op jit(solution)/shard_map/pallas_call | solution.py:416
  43.4 1.6 %copy.11 = f32[128,256]{1,0:T(8,128)} copy(f32[128,256]{1,0:T(8,128)} %shard_map.91) | data formatting | bytes 262144

commit v6 on v5

--- a/solution.py
+++ b/solution.py
@@ -26,46 +26,51 @@
 
 def compute_kernel(
     hi_lane,
-    ci_ref,
-    one_ref,
-    pair_ref,
-    bt_ref,
-    bp_ref,
-    bs_ref,
-    at_ref,
-    ap_ref,
-    as_ref,
-    out_ref,
-    rows_ref,
-    near_part_ref,
-    far_part_ref,
-    near_got_ref,
-    far_got_ref,
-    last_part_ref,
-    last_got_ref,
-    one_pad_ref,
-    pair_pad_ref,
-    code_ref,
-    turned_ref,
-    group_ref,
-    dens_ref,
-    sv_ref,
-    lift_ref,
-    lift_bf_ref,
-    wide_ref,
-    own_ref,
-    even_ref,
-    odd_ref,
-    order_ref,
-    beta_send,
-    beta_recv,
-    near_send,
-    near_recv,
-    far_send,
-    far_recv,
-    last_send,
-    last_recv,
+    *refs,
 ):
+    given, refs = refs[:9], refs[9:]
+    (
+        out_ref,
+        rows_ref,
+        near_part_ref,
+        far_part_ref,
+        near_got_ref,
+        far_got_ref,
+        last_part_ref,
+        last_got_ref,
+        one_pad_ref,
+        pair_pad_ref,
+        code_ref,
+        turned_ref,
+        group_ref,
+        dens_ref,
+        sv_ref,
+        lift_ref,
+        lift_bf_ref,
+        wide_ref,
+        own_ref,
+        even_ref,
+        odd_ref,
+        order_ref,
+        beta_send,
+        beta_recv,
+        near_send,
+        near_recv,
+        far_send,
+        far_recv,
+        last_send,
+        last_recv,
+        ci_ref,
+        one_ref,
+        pair_ref,
+        bt_ref,
+        bp_ref,
+        bs_ref,
+        at_ref,
+        ap_ref,
+        as_ref,
+        load_sem,
+    ) = refs
     blocks, rows, cols = rows_ref.shape
     excits = bt_ref.shape[0]
     slots = excits + 2
@@ -98,6 +103,14 @@
     for r in range(1, 4):
         for peer in (at_far(turned(mine, r)), at_near(turned(place, r))):
             pl.semaphore_signal(barrier, inc=1, device_id=peer, device_id_type=MESH)
+    kept = (ci_ref, bt_ref, bp_ref, bs_ref, at_ref, ap_ref, as_ref, one_ref, pair_ref)
+    order = (0, 3, 4, 5, 6, 7, 8, 1, 2)
+    loads = [
+        pltpu.make_async_copy(given[n], kept[k], load_sem.at[k]) for k, n in enumerate(order)
+    ]
+    for load in loads:
+        load.start()
+    loads[0].wait()
     rows_ref[me_beta] = ci_ref[...].astype(BF)
     pl.semaphore_wait(barrier, len(beta_peers) + 6)
 
@@ -176,6 +189,9 @@
     for k in range(4):
         sends[k].start()
 
+    for load in loads[1:]:
+        load.wait()
+
     code_ref[...] = jnp.zeros_like(code_ref)
     listed = bt_ref[...] + 2048 * bp_ref[...] + (1 << 18) * bs_ref[...]
     code_ref[0:excits, :] = listed.astype(F32)
@@ -317,7 +333,7 @@
             lift_ref[half, pl.ds(a, 48, stride=LS), :] = out[:, half * LANES : (half + 1) * LANES]
         return carry
 
-    lax.fori_loop(0, rows, lift_step, 0, unroll=16)
+    lax.fori_loop(0, rows, lift_step, 0, unroll=32)
     for half in range(2):
         at_half = slice(half * LANES, (half + 1) * LANES)
         for e in range(excits):
@@ -416,7 +432,7 @@
     return pl.pallas_call(
         functools.partial(compute_kernel, pairs),
         out_shape=jax.ShapeDtypeStruct((rows, cols), F32),
-        in_specs=[vmem] * 9,
+        in_specs=[pl.BlockSpec(memory_space=pltpu.HBM)] * 9,
         out_specs=vmem,
         scratch_shapes=[
             pltpu.VMEM((blocks, rows, cols), BF),
@@ -448,6 +464,16 @@
             pltpu.SemaphoreType.DMA((4, 4)),
             pltpu.SemaphoreType.DMA((2, 4)),
             pltpu.SemaphoreType.DMA((2, 4)),
+            pltpu.VMEM((rows, cols), F32),
+            pltpu.VMEM((1, pairs), F32),
+            pltpu.VMEM((pairs, pairs), BF),
+            pltpu.VMEM((excits, cols), jnp.int32),
+            pltpu.VMEM((excits, cols), jnp.int32),
+            pltpu.VMEM((excits, cols), jnp.int32),
+            pltpu.VMEM((excits, rows), jnp.int32),
+            pltpu.VMEM((excits, rows), jnp.int32),
+            pltpu.VMEM((excits, rows), jnp.int32),
+            pltpu.SemaphoreType.DMA((9,)),
         ],
         compiler_params=pltpu.CompilerParams(
             vmem_limit_bytes=56 * 2**20, collective_id=0, has_side_effects=True

time: 45.1 us -> 43.7 us (0.969)
  Pallas kernels: 43.4 us -> 42 us
    pallas_call x1, Pallas kernels: 43.4 us -> 42 us  [shards(): pl.pallas_call(functools.partial(compute_kernel, pairs), out_shape=jax.Sh...]
where the time goes in v6:
time: 43.7 us; the launch traced here: 43.6 us
  Pallas kernels  42 us (96%)
  local copies, waits for them, and re-layouts  1.57 us (4%)
    pallas_call x1, Pallas kernels, shards(): pl.pallas_call(functools.partial(compute_kernel, pairs), out_shape=jax.Sh...  42 us
    unnamed x1, local copies, waits for them, and re-layouts  1.57 us

profile of v6, /device:TPU:1, one launch (start us, length us, event | category | flops | bytes accessed | tf_op | source)
XLA Modules:
  0.0 43.6 jit_solution(12971881733187857386)
XLA Ops:
  0.0 42.0 %shard_map.91 = f32[128,256]{1,0:T(8,128)} custom-call(f32[128,256]{1,0:T(8,128)} %refs_0_.1, f32[1,102]{1,0:T(1,128)} %bitcast.1, bf16[102,102]{1,0:T(8,128)(2,1)} %refs_2_.1, s32[40,256]{1,0:T(8,128)} %refs_3_.1, s32[40,256]{1,0:T(8,128)} %refs_4_.1, s32[40,256]{1,0:T(8,128)} %refs_5_.1, s32[40,128]{1,0:T(8,128)} %refs_6_.1, s32[40,128]{1,0:T(8,128)} %refs_7_.1, ...), custom_call_target="tpu_custom_call" | custom-call | tf_op jit(solution)/shard_map/pallas_call | solution.py:432
  42.0 1.6 %copy.11 = f32[128,256]{1,0:T(8,128)} copy(f32[128,256]{1,0:T(8,128)} %shard_map.91) | data formatting | bytes 262144

commit v7 on v6

--- a/solution.py
+++ b/solution.py
@@ -17,7 +17,7 @@
 DS = 132
 SS = 136
 LS = 136
-BATCH = 4
+BATCH = 11
 
 
 def iota(shape, dim):

time: 43.7 us -> 43 us (0.984)
  Pallas kernels: 42 us -> 41.3 us
    pallas_call x1, Pallas kernels: 42 us -> 41.3 us  [shards(): pl.pallas_call(functools.partial(compute_kernel, pairs), out_shape=jax.Sh...]
where the time goes in v7:
time: 43 us; the launch traced here: 42.9 us
  Pallas kernels  41.3 us (96%)
  local copies, waits for them, and re-layouts  1.57 us (4%)
    pallas_call x1, Pallas kernels, shards(): pl.pallas_call(functools.partial(compute_kernel, pairs), out_shape=jax.Sh...  41.3 us
    unnamed x1, local copies, waits for them, and re-layouts  1.57 us

profile of v7, /device:TPU:1, one launch (start us, length us, event | category | flops | bytes accessed | tf_op | source)
XLA Modules:
  0.0 42.9 jit_solution(5276766782192454744)
XLA Ops:
  0.0 41.3 %shard_map.91 = f32[128,256]{1,0:T(8,128)} custom-call(f32[128,256]{1,0:T(8,128)} %refs_0_.1, f32[1,102]{1,0:T(1,128)} %bitcast.1, bf16[102,102]{1,0:T(8,128)(2,1)} %refs_2_.1, s32[40,256]{1,0:T(8,128)} %refs_3_.1, s32[40,256]{1,0:T(8,128)} %refs_4_.1, s32[40,256]{1,0:T(8,128)} %refs_5_.1, s32[40,128]{1,0:T(8,128)} %refs_6_.1, s32[40,128]{1,0:T(8,128)} %refs_7_.1, ...), custom_call_target="tpu_custom_call" | custom-call | tf_op jit(solution)/shard_map/pallas_call | solution.py:432
  41.3 1.6 %copy.11 = f32[128,256]{1,0:T(8,128)} copy(f32[128,256]{1,0:T(8,128)} %shard_map.91) | data formatting | bytes 262144

commit v8 on v7

--- a/solution.py
+++ b/solution.py
@@ -333,7 +333,7 @@
             lift_ref[half, pl.ds(a, 48, stride=LS), :] = out[:, half * LANES : (half + 1) * LANES]
         return carry
 
-    lax.fori_loop(0, rows, lift_step, 0, unroll=32)
+    lax.fori_loop(0, rows, lift_step, 0, unroll=64)
     for half in range(2):
         at_half = slice(half * LANES, (half + 1) * LANES)
         for e in range(excits):

time: 43 us -> 42.8 us (level)
  no operation moved by 1% of the time
where the time goes in v8:
time: 42.8 us; the launch traced here: 42.6 us
  Pallas kernels  41.1 us (96%)
  local copies, waits for them, and re-layouts  1.57 us (4%)
    pallas_call x1, Pallas kernels, shards(): pl.pallas_call(functools.partial(compute_kernel, pairs), out_shape=jax.Sh...  41.1 us
    unnamed x1, local copies, waits for them, and re-layouts  1.57 us

profile of v8, /device:TPU:1, one launch (start us, length us, event | category | flops | bytes accessed | tf_op | source)
XLA Modules:
  0.0 42.6 jit_solution(18046204102113798493)
XLA Ops:
  0.0 41.1 %shard_map.91 = f32[128,256]{1,0:T(8,128)} custom-call(f32[128,256]{1,0:T(8,128)} %refs_0_.1, f32[1,102]{1,0:T(1,128)} %bitcast.1, bf16[102,102]{1,0:T(8,128)(2,1)} %refs_2_.1, s32[40,256]{1,0:T(8,128)} %refs_3_.1, s32[40,256]{1,0:T(8,128)} %refs_4_.1, s32[40,256]{1,0:T(8,128)} %refs_5_.1, s32[40,128]{1,0:T(8,128)} %refs_6_.1, s32[40,128]{1,0:T(8,128)} %refs_7_.1, ...), custom_call_target="tpu_custom_call" | custom-call | tf_op jit(solution)/shard_map/pallas_call | solution.py:432
  41.1 1.6 %copy.11 = f32[128,256]{1,0:T(8,128)} copy(f32[128,256]{1,0:T(8,128)} %shard_map.91) | data formatting | bytes 262144
